TPU v7x, 32 devices: a whole 2x2x4 slice. The times are simulated.
32 devices in a mesh: section: 2 (over core), ctx: 4 (over y, x), tp: 4 (over z).
Axes of the slice: x: 2, y: 2, z: 4, core: 2. Of those that a mesh axis runs over, the one named last changes fastest.
Arguments:
- inputs: bfloat16 [2, 2, 1024, 2048], P(None, None, 'ctx'), may hold values from -6 to 6
- grad_out: float32 [2, 2, 1024, 2048], P(None, None, 'ctx'), may hold values from -6 to 6
- ln1_gain: bfloat16 [2, 2048], P('section', 'ctx'), may hold values from 0.5 to 1.5
- ln1_bias: bfloat16 [2, 2048], P('section', 'ctx'), may hold values from -3 to 3
- ln2_gain: bfloat16 [2, 2048], P('section', 'ctx'), may hold values from 0.5 to 1.5
- ln2_bias: bfloat16 [2, 2048], P('section', 'ctx'), may hold values from -3 to 3
- w_qkv: bfloat16 [2, 2048, 8, 768], P('section', 'ctx', 'tp'), may hold values from -0.125 to 0.125
- qkv_bias: bfloat16 [2, 8, 768], P('section', 'tp', 'ctx'), may hold values from -3 to 3
- w_dense: bfloat16 [2, 2048, 2048], P('section', 'tp', 'ctx'), may hold values from -1.5 to 1.5
- w_up: bfloat16 [2, 2048, 8192], P('section', 'ctx', 'tp'), may hold values from -0.125 to 0.125
- up_bias: bfloat16 [2, 8192], P('section', ('tp', 'ctx')), may hold values from -3 to 3
- w_down: bfloat16 [2, 8192, 2048], P('section', 'tp', 'ctx'), may hold values from -0.0625 to 0.0625
- out_bias: bfloat16 [2, 2048], P('section', 'ctx'), may hold values from -3 to 3
Outputs:
- block_ends: float32 [2, 2, 2, 1024, 2048], P('section', None, None, 'ctx')
- grad_ln1_gain: float32 [2, 2048], P('section', 'ctx')
- grad_ln1_bias: float32 [2, 2048], P('section', 'ctx')
- grad_ln2_gain: float32 [2, 2048], P('section', 'ctx')
- grad_ln2_bias: float32 [2, 2048], P('section', 'ctx')
- grad_w_qkv: float32 [2, 2048, 8, 768], P('section', 'ctx', 'tp')
- grad_qkv_bias: float32 [2, 8, 768], P('section', 'tp', 'ctx')
- grad_w_dense: float32 [2, 2048, 2048], P('section', 'tp', 'ctx')
- grad_w_up: float32 [2, 2048, 8192], P('section', 'ctx', 'tp')
- grad_up_bias: float32 [2, 8192], P('section', ('tp', 'ctx'))
- grad_w_down: float32 [2, 8192, 2048], P('section', 'tp', 'ctx')
- grad_out_bias: float32 [2, 2048], P('section', 'ctx')
All inputs are finite; a program needn't handle non-finite values.
Results may differ from a plain program's by a relative error of at most 0.022.
Values may be sent and summed in bfloat16 or wider, within the bound.
A program may use at most 384 MiB of HBM per device.

v0:
```python
import math

import jax
import jax.numpy as jnp
from jax import lax
from jax.sharding import PartitionSpec as P

norm_eps = 1e-05
root_half = 1.0 / math.sqrt(2.0)
root_tau = 1.0 / math.sqrt(2.0 * math.pi)


def from_behind(shard, axis, by):
    size = lax.axis_size(axis)
    pairs = [(i, i + by) for i in range(size) if 0 <= i + by < size]
    return lax.ppermute(shard, axis, pairs)


def layer_norm(row_block, gain_vec, shift_vec):
    row_mean = jnp.mean(row_block, axis=-1, keepdims=True)
    centered = row_block - row_mean
    row_var = jnp.mean(centered * centered, axis=-1, keepdims=True)
    inverse = lax.rsqrt(row_var + norm_eps)
    unit_rows = centered * inverse
    return (unit_rows * gain_vec + shift_vec, unit_rows, inverse)


def norm_back(grad_rows, unit_rows, inverse, gain_vec):
    scaled = grad_rows * gain_vec
    first_mean = jnp.mean(scaled, axis=-1, keepdims=True)
    second_mean = jnp.mean(scaled * unit_rows, axis=-1, keepdims=True)
    return inverse * (scaled - first_mean - unit_rows * second_mean)


def gelu_parts(values):
    normal_cdf = 0.5 * (1.0 + lax.erf(values * root_half))
    return (values * normal_cdf, normal_cdf + values * jnp.exp(-0.5 * values * values) * root_tau)


def rotary_tables(positions, rot_width):
    half_width = rot_width // 2
    frequency = jnp.exp(
        jnp.arange(half_width).astype(jnp.float32) * (-2.0 * math.log(10000.0) / rot_width)
    )
    angles = positions[:, None] * frequency[None, :]
    cosine = jnp.cos(angles)
    sine = jnp.sin(angles)
    return (
        jnp.concatenate([cosine, cosine], -1)[:, None, :],
        jnp.concatenate([sine, sine], -1)[:, None, :],
    )


def rotate_heads(features, cosine, sine):
    rot_width = cosine.shape[-1]
    half_width = rot_width // 2
    rotated_part = features[..., :rot_width]
    turned = jnp.concatenate([-rotated_part[..., half_width:], rotated_part[..., :half_width]], -1)
    return jnp.concatenate([rotated_part * cosine + turned * sine, features[..., rot_width:]], -1)


def rotate_back(grads, cosine, sine):
    rot_width = cosine.shape[-1]
    half_width = rot_width // 2
    rotated_part = grads[..., :rot_width]
    weighted = rotated_part * sine
    turned = jnp.concatenate([weighted[..., half_width:], -weighted[..., :half_width]], -1)
    return jnp.concatenate([rotated_part * cosine + turned, grads[..., rot_width:]], -1)


def dot_transposed(left, right):
    return lax.dot_general(
        left, right, (((1,), (1,)), ((), ())), preferred_element_type=jnp.float32
    )


def transposed_dot(left, right):
    return lax.dot_general(
        left, right, (((0,), (0,)), ((), ())), preferred_element_type=jnp.float32
    )


def pack_terms(term_list, axis_list, shard_count):
    flat_list = []
    shape_list = []
    for term_value, axis_pos in zip(term_list, axis_list):
        moved_term = jnp.moveaxis(term_value, axis_pos, 0)
        shape_list.append(moved_term.shape)
        flat_list.append(moved_term.reshape(shard_count, -1))
    return (jnp.concatenate(flat_list, 1), shape_list)


def unpack_terms(packed, shape_list, axis_list, shard_count):
    result_list = []
    offset = 0
    for shape_now, axis_pos in zip(shape_list, axis_list):
        span_size = math.prod(shape_now) // shard_count
        piece_part = packed[:, offset : offset + span_size].reshape(
            (shape_now[0] // shard_count,) + tuple(shape_now[1:])
        )
        result_list.append(jnp.moveaxis(piece_part, 0, axis_pos))
        offset = offset + span_size
    return tuple(result_list)


def masked_scores(query_rows, key_all, allowed, score_scale):
    scores = (
        jnp.einsum("sqhd,skhd->shqk", query_rows, key_all, preferred_element_type=jnp.float32)
        * score_scale
    )
    return jnp.where(allowed, scores, -1e30)


def attend_heads(query_rows, key_all, value_all, allowed, score_scale):
    scores = masked_scores(query_rows, key_all, allowed, score_scale)
    row_top = jnp.max(scores, axis=-1, keepdims=True)
    row_total = jnp.sum(jnp.exp(scores - row_top), axis=-1, keepdims=True)
    log_total = row_top + jnp.log(row_total)
    probabilities = jnp.where(allowed, jnp.exp(scores - log_total), 0.0)
    context = jnp.einsum(
        "shqk,skhd->sqhd",
        probabilities.astype(jnp.bfloat16),
        value_all,
        preferred_element_type=jnp.float32,
    ).astype(jnp.bfloat16)
    return (context, log_total)


def attend_back(
    query_rows, key_all, value_all, context, log_total, grad_context, allowed, score_scale
):
    scores = masked_scores(query_rows, key_all, allowed, score_scale)
    probabilities = jnp.where(allowed, jnp.exp(scores - log_total), 0.0)
    grad_half = grad_context.astype(jnp.bfloat16)
    row_delta = jnp.sum(grad_context * context.astype(jnp.float32), axis=-1).transpose(0, 2, 1)[
        ..., None
    ]
    grad_probs = jnp.einsum(
        "sqhd,skhd->shqk", grad_half, value_all, preferred_element_type=jnp.float32
    )
    grad_scores = (probabilities * (grad_probs - row_delta)).astype(jnp.bfloat16)
    grad_query = (
        jnp.einsum("shqk,skhd->sqhd", grad_scores, key_all, preferred_element_type=jnp.float32)
        * score_scale
    )
    grad_key = (
        jnp.einsum("shqk,sqhd->skhd", grad_scores, query_rows, preferred_element_type=jnp.float32)
        * score_scale
    )
    grad_value = jnp.einsum(
        "shqk,sqhd->skhd",
        probabilities.astype(jnp.bfloat16),
        grad_half,
        preferred_element_type=jnp.float32,
    )
    return (grad_query, grad_key, grad_value)


def on_device(
    inputs,
    grad_out,
    ln1_gain,
    ln1_bias,
    ln2_gain,
    ln2_bias,
    w_qkv,
    qkv_bias,
    w_dense,
    w_up,
    up_bias,
    w_down,
    out_bias,
):
    section_index = lax.axis_index("section")
    context_index = lax.axis_index("ctx")
    ctx_count = lax.axis_size("ctx")
    micro_count, seq_count, tok_rows, model_width = inputs.shape
    seq_length = tok_rows * ctx_count
    head_count = w_qkv.shape[2]
    head_dim = w_qkv.shape[3] // 3
    score_scale = 1.0 / math.sqrt(head_dim)
    flat_count = seq_count * tok_rows
    grad_dims = (0, 0, 0, 0, 0, 1, 1, 0, 0, 1, 0)
    gathered = (
        lax.all_gather(ln1_gain, "ctx", axis=1, tiled=True),
        lax.all_gather(ln1_bias, "ctx", axis=1, tiled=True),
        lax.all_gather(ln2_gain, "ctx", axis=1, tiled=True),
        lax.all_gather(ln2_bias, "ctx", axis=1, tiled=True),
        lax.all_gather(w_qkv, "ctx", axis=1, tiled=True),
        lax.all_gather(qkv_bias, "ctx", axis=2, tiled=True),
        lax.all_gather(w_dense, "ctx", axis=2, tiled=True),
        lax.all_gather(w_up, "ctx", axis=1, tiled=True),
        lax.all_gather(up_bias, "ctx", axis=1, tiled=True),
        lax.all_gather(w_down, "ctx", axis=2, tiled=True),
        lax.all_gather(out_bias, "ctx", axis=1, tiled=True),
    )
    gain_one = gathered[0][0].astype(jnp.float32)
    bias_one = gathered[1][0].astype(jnp.float32)
    gain_two = gathered[2][0].astype(jnp.float32)
    bias_two = gathered[3][0].astype(jnp.float32)
    qkv_full = gathered[4][0].reshape(model_width, head_count * 3 * head_dim)
    qkv_shift = gathered[5][0].astype(jnp.float32).reshape(head_count * 3 * head_dim)
    dense_full = gathered[6][0]
    up_full = gathered[7][0]
    up_shift = gathered[8][0].astype(jnp.float32)
    down_full = gathered[9][0]
    out_shift = gathered[10][0].astype(jnp.float32)
    query_index = context_index * tok_rows + jnp.arange(tok_rows, dtype=jnp.int32)
    allowed = jnp.arange(seq_length, dtype=jnp.int32)[None, :] <= query_index[:, None]
    cosine, sine = rotary_tables(query_index.astype(jnp.float32), head_dim // 4)
    received = jnp.zeros((seq_count, tok_rows, model_width), jnp.bfloat16)
    saved_steps = []
    outputs = []
    for turn_index in range(micro_count + 1):
        fresh_rows = inputs[min(turn_index, micro_count - 1)]
        layer_rows = jnp.where(section_index == 0, fresh_rows, received)
        flat_rows = layer_rows.reshape(flat_count, model_width).astype(jnp.float32)
        normed_one, layer_unit_one, layer_inverse_one = layer_norm(flat_rows, gain_one, bias_one)
        normed_two, layer_unit_two, layer_inverse_two = layer_norm(flat_rows, gain_two, bias_two)
        layer_input_one = normed_one.astype(jnp.bfloat16)
        layer_input_two = normed_two.astype(jnp.bfloat16)
        mixed_rows = (
            jnp.dot(layer_input_one, qkv_full, preferred_element_type=jnp.float32) + qkv_shift
        )
        mixed_rows = mixed_rows.reshape(seq_count, tok_rows, head_count, 3 * head_dim)
        layer_query_rows = rotate_heads(mixed_rows[..., :head_dim], cosine, sine).astype(
            jnp.bfloat16
        )
        layer_key_rows = rotate_heads(
            mixed_rows[..., head_dim : 2 * head_dim], cosine, sine
        ).astype(jnp.bfloat16)
        layer_value_rows = mixed_rows[..., 2 * head_dim :].astype(jnp.bfloat16)
        layer_key_all = lax.all_gather(layer_key_rows, "ctx", axis=1, tiled=True)
        layer_value_all = lax.all_gather(layer_value_rows, "ctx", axis=1, tiled=True)
        layer_context, layer_log_total = attend_heads(
            layer_query_rows, layer_key_all, layer_value_all, allowed, score_scale
        )
        pre_act = jnp.dot(layer_input_two, up_full, preferred_element_type=jnp.float32) + up_shift
        activated, layer_slope = gelu_parts(pre_act)
        layer_active = activated.astype(jnp.bfloat16)
        partial_sum = jnp.dot(
            layer_context.reshape(flat_count, head_count * head_dim),
            dense_full,
            preferred_element_type=jnp.float32,
        )
        partial_sum = partial_sum + jnp.dot(
            layer_active, down_full, preferred_element_type=jnp.float32
        )
        branch = lax.psum(partial_sum.astype(jnp.bfloat16), "tp").astype(jnp.float32)
        result = (flat_rows + branch + out_shift).reshape(seq_count, tok_rows, model_width)
        layer_kept_keys = ()
        result, saved_state = (
            result,
            (
                layer_unit_one,
                layer_inverse_one,
                layer_unit_two,
                layer_inverse_two,
                layer_input_one,
                layer_input_two,
                layer_query_rows,
                layer_key_rows,
                layer_value_rows,
                layer_kept_keys,
                layer_context,
                layer_log_total,
                layer_slope,
                layer_active,
            ),
        )
        saved_steps.append(saved_state)
        outputs.append(result)
        if turn_index < micro_count:
            sending = result.astype(jnp.bfloat16)
            received = from_behind(sending, "section", 1)
    received_grad = jnp.zeros((seq_count, tok_rows, model_width), jnp.float32)
    grad_inputs = []
    totals = None
    for turn_index in range(micro_count + 1):
        fresh_grad = grad_out[min(turn_index, micro_count - 1)]
        grads_in = jnp.where(section_index == 1, fresh_grad, received_grad)
        saved_state = jax.tree.map(
            lambda later_value, early_value: jnp.where(
                section_index == 1, later_value, early_value
            ),
            saved_steps[min(turn_index + 1, micro_count)],
            saved_steps[max(turn_index - 1, 0)],
        )
        is_valid = jnp.where(section_index == 1, turn_index < micro_count, turn_index >= 1)
        (
            unit_one,
            inverse_one,
            unit_two,
            inverse_two,
            input_one,
            input_two,
            query_rows,
            key_rows,
            value_rows,
            kept_keys,
            context,
            log_total,
            slope,
            active,
        ) = saved_state
        key_all = lax.all_gather(key_rows, "ctx", axis=1, tiled=True)
        value_all = lax.all_gather(value_rows, "ctx", axis=1, tiled=True)
        grad_flat = grads_in.reshape(flat_count, model_width)
        grad_half = grad_flat.astype(jnp.bfloat16)
        grad_out_shift = jnp.sum(grad_flat, 0)
        grad_down = transposed_dot(active, grad_half)
        grad_pre = dot_transposed(grad_half, down_full) * slope
        grad_up_shift = jnp.sum(grad_pre, 0)
        pre_half = grad_pre.astype(jnp.bfloat16)
        grad_up = transposed_dot(input_two, pre_half)
        back_two = dot_transposed(pre_half, up_full)
        grad_dense = transposed_dot(context.reshape(flat_count, head_count * head_dim), grad_half)
        grad_context = dot_transposed(grad_half, dense_full).reshape(
            seq_count, tok_rows, head_count, head_dim
        )
        grad_query, grad_key_all, grad_value_all = attend_back(
            query_rows, key_all, value_all, context, log_total, grad_context, allowed, score_scale
        )
        key_value_grads = lax.psum_scatter(
            jnp.stack([grad_key_all, grad_value_all]).astype(jnp.bfloat16),
            "ctx",
            scatter_dimension=2,
            tiled=True,
        ).astype(jnp.float32)
        grad_key = key_value_grads[0]
        grad_value = key_value_grads[1]
        grad_mixed = jnp.concatenate(
            [
                rotate_back(grad_query, cosine, sine),
                rotate_back(grad_key, cosine, sine),
                grad_value,
            ],
            -1,
        )
        grad_qkv_shift = jnp.sum(grad_mixed, (0, 1))
        mixed_half = grad_mixed.reshape(flat_count, head_count * 3 * head_dim).astype(jnp.bfloat16)
        grad_qkv = transposed_dot(input_one, mixed_half).reshape(
            model_width, head_count, 3 * head_dim
        )
        back_one = dot_transposed(mixed_half, qkv_full)
        back_one, back_two = (
            lax.psum(back_one.astype(jnp.bfloat16), "tp").astype(jnp.float32),
            lax.psum(back_two.astype(jnp.bfloat16), "tp").astype(jnp.float32),
        )
        grad_gain_one = jnp.sum(back_one * unit_one, 0)
        grad_bias_one = jnp.sum(back_one, 0)
        grad_gain_two = jnp.sum(back_two * unit_two, 0)
        grad_bias_two = jnp.sum(back_two, 0)
        grad_input = (
            grad_flat
            + norm_back(back_one, unit_one, inverse_one, gain_one)
            + norm_back(back_two, unit_two, inverse_two, gain_two)
        )
        grad_terms = (
            grad_gain_one,
            grad_bias_one,
            grad_gain_two,
            grad_bias_two,
            grad_qkv,
            grad_qkv_shift,
            grad_dense,
            grad_up,
            grad_up_shift,
            grad_down,
            grad_out_shift,
        )
        grad_rows, grad_terms = (grad_input.reshape(seq_count, tok_rows, model_width), grad_terms)
        grad_terms = tuple((jnp.where(is_valid, term_value, 0.0) for term_value in grad_terms))
        if totals is None:
            totals = tuple(grad_terms)
        else:
            totals = tuple((left + right for left, right in zip(totals, grad_terms)))
        grad_inputs.append(grad_rows)
        if turn_index < micro_count:
            received_grad = from_behind(grad_rows.astype(jnp.bfloat16), "section", -1).astype(
                grad_rows.dtype
            )
    packed, shape_list = pack_terms(totals, grad_dims, ctx_count)
    packed = lax.psum_scatter(
        packed.astype(jnp.bfloat16), "ctx", scatter_dimension=0, tiled=True
    ).astype(jnp.float32)
    totals = unpack_terms(packed, shape_list, grad_dims, ctx_count)
    block_ends = jnp.where(section_index == 1, jnp.stack(outputs[1:]), jnp.stack(grad_inputs[1:]))[
        None
    ]
    return (
        block_ends,
        totals[0][None],
        totals[1][None],
        totals[2][None],
        totals[3][None],
        totals[4][None],
        totals[5][None],
        totals[6][None],
        totals[7][None],
        totals[8][None],
        totals[9][None],
        totals[10][None],
    )


def solution(mesh):
    placed = (
        P(None, None, "ctx", None),
        P(None, None, "ctx", None),
        P("section", "ctx"),
        P("section", "ctx"),
        P("section", "ctx"),
        P("section", "ctx"),
        P("section", "ctx", "tp", None),
        P("section", "tp", "ctx"),
        P("section", "tp", "ctx"),
        P("section", "ctx", "tp"),
        P("section", ("tp", "ctx")),
        P("section", "tp", "ctx"),
        P("section", "ctx"),
    )
    return jax.shard_map(
        on_device,
        mesh=mesh,
        in_specs=placed,
        out_specs=(
            P("section", None, None, "ctx", None),
            P("section", "ctx"),
            P("section", "ctx"),
            P("section", "ctx"),
            P("section", "ctx"),
            P("section", "ctx", "tp", None),
            P("section", "tp", "ctx"),
            P("section", "tp", "ctx"),
            P("section", "ctx", "tp"),
            P("section", ("tp", "ctx")),
            P("section", "tp", "ctx"),
            P("section", "ctx"),
        ),
        check_vma=False,
    )
```

profile of v0, /device:TPU:0, one launch (start us, length us, event | category | flops | bytes accessed | tf_op | source)
XLA Modules:
  0.0 2450.3 jit_solution(13096860137690624392)
XLA Ops:
  61.9 22.4 all-gather.17.cloned.1.call-done
  116.4 23.3 all-gather.21.cloned.1.call-done
  145.1 32.3 %all-gather.19.cloned.1.call-done = bf16[2,1024,2,256]{3,1,2,0:T(8,128)(2,1)} async-done(((bf16[2,256,2,256]{3,1,2,0:T(8,128)(2,1)}), bf16[2,1024,2,256]{3,1,2,0:T(8,128)(2,1)}) %all-gather.19.cloned.1.call-update) | async-done | bytes 2097168 | tf_op jit(solution)/shard_map/all_gather | solution.py:234
  182.7 84.1 %all-gather.25.cloned.1.call-done = bf16[1,2048,2048]{2,1,0:T(8,128)(2,1)} async-done(((bf16[1,512,2048]{2,1,0:T(8,128)(2,1)}), bf16[1,2048,2048]{2,1,0:T(8,128)(2,1)}) %all-gather.25.cloned.1.call-update) | async-done | bytes 8388624 | tf_op jit(solution)/shard_map/all_gather | solution.py:192
  277.5 78.4 %all-gather.27.cloned.1.call-done = bf16[1,2048,2048]{2,1,0:T(8,128)(2,1)} async-done(((bf16[1,2048,512]{2,1,0:T(8,128)(2,1)}), bf16[1,2048,2048]{2,1,0:T(8,128)(2,1)}) %all-gather.27.cloned.1.call-update) | async-done | bytes 8388624 | tf_op jit(solution)/shard_map/all_gather | solution.py:194
  367.1 25.7 %all-gather.23.cloned.1.call-done = bf16[1,512,2048]{2,1,0:T(8,128)(2,1)} async-done(((bf16[1,512,512]{2,1,0:T(8,128)(2,1)}), bf16[1,512,2048]{2,1,0:T(8,128)(2,1)}) %all-gather.23.cloned.1.call-update) | async-done | bytes 2097168 | tf_op jit(solution)/shard_map/all_gather | solution.py:191
  406.6 78.4 %all-reduce.10.cloned.1.call-done = bf16[512,2048]{1,0:T(8,128)(2,1)} async-done(((bf16[512,2048]{1,0:T(8,128)(2,1)}), bf16[512,2048]{1,0:T(8,128)(2,1)}) %all-reduce.10.cloned.1.call-update) | async-done | bytes 2097168 | tf_op jit(solution)/shard_map/psum | solution.py:249
  539.1 14.7 all-gather.31.cloned.1.call-done
  558.4 33.3 %all-gather.37.cloned.1.call-done = bf16[2,1024,2,256]{3,1,2,0:T(8,128)(2,1)} async-done(((bf16[2,256,2,256]{3,1,2,0:T(8,128)(2,1)}), bf16[2,1024,2,256]{3,1,2,0:T(8,128)(2,1)}) %all-gather.37.cloned.1.call-update) | async-done | bytes 2097168 | tf_op jit(solution)/shard_map/all_gather | solution.py:306
  599.1 29.7 %all-gather.29.cloned.1.call-done = bf16[2,1024,2,256]{3,1,2,0:T(8,128)(2,1)} async-done(((bf16[2,256,2,256]{3,1,2,0:T(8,128)(2,1)}), bf16[2,1024,2,256]{3,1,2,0:T(8,128)(2,1)}) %all-gather.29.cloned.1.call-update) | async-done | bytes 2097168 | tf_op jit(solution)/shard_map/all_gather | solution.py:234
  634.7 31.5 %all-gather.39.cloned.1.call-done = bf16[2,1024,2,256]{3,1,2,0:T(8,128)(2,1)} async-done(((bf16[2,256,2,256]{3,1,2,0:T(8,128)(2,1)}), bf16[2,1024,2,256]{3,1,2,0:T(8,128)(2,1)}) %all-gather.39.cloned.1.call-update) | async-done | bytes 2097168 | tf_op jit(solution)/shard_map/all_gather | solution.py:307
  684.7 13.0 fusion.321
  754.4 223.0 %all-reduce.18.cloned.1.call-done = (bf16[512,2048]{1,0:T(8,128)(2,1)}, bf16[512,2048]{1,0:T(8,128)(2,1)}, bf16[512,2048]{1,0:T(8,128)(2,1)}) async-done(((bf16[512,2048]{1,0:T(8,128)(2,1)}, bf16[512,2048]{1,0:T(8,128)(2,1)}, bf16[512,2048]{1,0:T(8,128)(2,1)}), (bf16[512,2048]{1,0:T(8,128)(2,1)}, bf16[512,2048]{1,0:T(8,128)(2,1)}, bf16[512,2048]{1,0:T(8,128)(2,1)})) %all-reduce.18.cloned.1.call-update) | async-done | bytes 6291472 | tf_op jit(solution)/shard_map/psum | solution.py:249
  1056.2 32.4 %all-gather.41.cloned.1.call-done = bf16[2,1024,2,256]{3,1,2,0:T(8,128)(2,1)} async-done(((bf16[2,256,2,256]{3,1,2,0:T(8,128)(2,1)}), bf16[2,1024,2,256]{3,1,2,0:T(8,128)(2,1)}) %all-gather.41.cloned.1.call-update) | async-done | bytes 2097168 | tf_op jit(solution)/shard_map/all_gather | solution.py:306
  1096.1 29.6 %all-gather.33.cloned.1.call-done = bf16[2,1024,2,256]{3,1,2,0:T(8,128)(2,1)} async-done(((bf16[2,256,2,256]{3,1,2,0:T(8,128)(2,1)}), bf16[2,1024,2,256]{3,1,2,0:T(8,128)(2,1)}) %all-gather.33.cloned.1.call-update) | async-done | bytes 2097168 | tf_op jit(solution)/shard_map/all_gather | solution.py:234
  1131.5 31.2 %all-gather.43.cloned.1.call-done = bf16[2,1024,2,256]{3,1,2,0:T(8,128)(2,1)} async-done(((bf16[2,256,2,256]{3,1,2,0:T(8,128)(2,1)}), bf16[2,1024,2,256]{3,1,2,0:T(8,128)(2,1)}) %all-gather.43.cloned.1.call-update) | async-done | bytes 2097168 | tf_op jit(solution)/shard_map/all_gather | solution.py:307
  1181.0 13.0 fusion.320
  1202.0 23.5 reduce-scatter.6.cloned.1.call-done
  1251.2 154.8 %all-reduce.16.cloned.1.call-done = (bf16[512,2048]{1,0:T(8,128)(2,1)}, bf16[512,2048]{1,0:T(8,128)(2,1)}) async-done(((bf16[512,2048]{1,0:T(8,128)(2,1)}, bf16[512,2048]{1,0:T(8,128)(2,1)}), (bf16[512,2048]{1,0:T(8,128)(2,1)}, bf16[512,2048]{1,0:T(8,128)(2,1)})) %all-reduce.16.cloned.1.call-update) | async-done | bytes 4194320 | tf_op jit(solution)/shard_map/psum | solution.py:348
  1489.7 12.8 fusion.182
  1593.0 14.0 add_convert_fusion
  1606.9 13.2 reshape.843
  1632.0 13.1 copy.455
  1655.2 143.5 %all-reduce.14.cloned.1.call-done = (bf16[512,2048]{1,0:T(8,128)(2,1)}, bf16[512,2048]{1,0:T(8,128)(2,1)}, bf16[512,2048]{1,0:T(8,128)(2,1)}) async-done(((bf16[512,2048]{1,0:T(8,128)(2,1)}, bf16[512,2048]{1,0:T(8,128)(2,1)}, bf16[512,2048]{1,0:T(8,128)(2,1)}), (bf16[512,2048]{1,0:T(8,128)(2,1)}, bf16[512,2048]{1,0:T(8,128)(2,1)}, bf16[512,2048]{1,0:T(8,128)(2,1)})) %all-reduce.14.cloned.1.call-update) | async-done | bytes 6291472 | tf_op jit(solution)/shard_map/psum | solution.py:249
  1809.7 12.8 fusion.179
  1822.5 12.1 add_convert_fusion.1
  1834.6 13.2 reshape.842
  1885.5 428.1 %all-reduce.12.cloned.1.call-done = bf16[4,3149184]{1,0:T(4,128)(2,1)} async-done(((bf16[4,3149184]{1,0:T(4,128)(2,1)}), bf16[4,3149184]{1,0:T(4,128)(2,1)}) %all-reduce.12.cloned.1.call-update) | async-done | bytes 25193488
  2313.7 14.2 dynamic-slice_convert_fusion
  2328.6 32.9 %slice_reduce_fusion.2 = f32[786432]{0:T(1024)S(1)} fusion(f32[1,3149184]{1,0:T(1,128)S(1)} %dynamic-slice_convert_fusion), kind=kLoop, calls=%fused_computation.222 | loop fusion | bytes 6291456 | tf_op jit(solution)/shard_map/slice | solution.py:98
  2361.5 11.8 slice_reduce_fusion.3
  2373.3 48.5 %slice_reduce_fusion = (f32[1048576]{0:T(1024)}, f32[1048576]{0:T(1024)}) fusion(f32[1,3149184]{1,0:T(1,128)} %copy-done.7), kind=kLoop, calls=%fused_computation.111 | loop fusion | bytes 16777216 | tf_op jit(solution)/shard_map/slice | solution.py:98
  (658 shorter events, 689.2 us)
Async XLA Ops:
  7.2 77.2 %all-gather.17.cloned.1.call-start = ((), (), s32[]{:S(2)}) async-start(), calls=%async_computation.3 | async-start | bytes 7864320 | tf_op jit(solution)/shard_map/all_gather | solution.py:189
  7.9 131.8 %all-gather.21.cloned.1.call-start = ((), (), s32[]{:S(2)}) async-start(), calls=%async_computation.5 | async-start | bytes 2621440 | tf_op jit(solution)/shard_map/all_gather | solution.py:233
  17.6 978.3 %copy-start.116 = (f32[1,2048]{1,0:T(1,128)}, f32[1,2048]{1,0:T(1,128)S(1)}, u32[]{:S(2)}) copy-start(f32[1,2048]{1,0:T(1,128)S(1)} %add.580) | copy-start | bytes 24580
  32.8 1140.1 %copy-start.114 = (f32[1,2048]{1,0:T(1,128)}, f32[1,2048]{1,0:T(1,128)S(1)}, u32[]{:S(2)}) copy-start(f32[1,2048]{1,0:T(1,128)S(1)} %add.581) | copy-start | bytes 24580
  40.8 1372.8 %copy-start.109 = (f32[1,2048]{1,0:T(1,128)}, f32[1,2048]{1,0:T(1,128)S(1)}, u32[]{:S(2)}) copy-start(f32[1,2048]{1,0:T(1,128)S(1)} %mul.792) | copy-start | bytes 24580
  104.0 73.4 %all-gather.19.cloned.1.call-start = ((), (), s32[]{:S(2)}) async-start(), calls=%async_computation.4 | async-start | bytes 2621440 | tf_op jit(solution)/shard_map/all_gather | solution.py:234
  106.0 160.8 %all-gather.25.cloned.1.call-start = ((), (), s32[]{:S(2)}) async-start(), calls=%async_computation.7 | async-start | bytes 10485760 | tf_op jit(solution)/shard_map/all_gather | solution.py:192
  106.6 249.4 %all-gather.27.cloned.1.call-start = ((), (), s32[]{:S(2)}) async-start(), calls=%async_computation.8 | async-start | bytes 10485760 | tf_op jit(solution)/shard_map/all_gather | solution.py:194
  107.2 285.7 %all-gather.23.cloned.1.call-start = ((), (), s32[]{:S(2)}) async-start(), calls=%async_computation.6 | async-start | bytes 2621440 | tf_op jit(solution)/shard_map/all_gather | solution.py:191
  107.7 377.2 %all-reduce.10.cloned.1.call-start = ((), (), s32[]{:S(2)}) async-start(), calls=%async_computation.9 | async-start | bytes 4194304 | tf_op jit(solution)/shard_map/psum | solution.py:249
  398.3 155.5 %all-gather.31.cloned.1.call-start = ((), (), s32[]{:S(2)}) async-start(), calls=%async_computation.11 | async-start | bytes 2621440 | tf_op jit(solution)/shard_map/all_gather | solution.py:233
  406.6 570.8 %copy-start.118 = (f32[1,2048]{1,0:T(1,128)}, f32[1,2048]{1,0:T(1,128)S(1)}, u32[]{:S(2)}) copy-start(f32[1,2048]{1,0:T(1,128)S(1)} %add.583) | copy-start | bytes 24580
  488.1 5.6 collective-permute-start
  518.4 73.2 %all-gather.37.cloned.1.call-start = ((), (), s32[]{:S(2)}) async-start(), calls=%async_computation.14 | async-start | bytes 2621440 | tf_op jit(solution)/shard_map/all_gather | solution.py:306
  519.2 109.7 %all-gather.29.cloned.1.call-start = ((), (), s32[]{:S(2)}) async-start(), calls=%async_computation.10 | async-start | bytes 2621440 | tf_op jit(solution)/shard_map/all_gather | solution.py:234
  521.6 144.6 %all-gather.39.cloned.1.call-start = ((), (), s32[]{:S(2)}) async-start(), calls=%async_computation.15 | async-start | bytes 2621440 | tf_op jit(solution)/shard_map/all_gather | solution.py:307
  527.2 201.8 %reduce-scatter.4.cloned.1.call-start = ((), (), s32[]{:S(2)}) async-start(), calls=%async_computation.16 | async-start | bytes 5242880 | tf_op jit(solution)/shard_map/reduce_scatter | solution.py:324
  676.2 301.2 %all-reduce.18.cloned.1.call-start = ((), (), s32[]{:S(2)}) async-start(), calls=%async_computation.26 | async-start | bytes 12582912 | tf_op jit(solution)/shard_map/psum | solution.py:249
  753.7 297.9 %all-gather.35.cloned.1.call-start = ((), (), s32[]{:S(2)}) async-start(), calls=%async_computation.13 | async-start | bytes 2621440 | tf_op jit(solution)/shard_map/all_gather | solution.py:233
  988.9 5.6 collective-permute-start.1
  1017.0 71.6 %all-gather.41.cloned.1.call-start = ((), (), s32[]{:S(2)}) async-start(), calls=%async_computation.17 | async-start | bytes 2621440 | tf_op jit(solution)/shard_map/all_gather | solution.py:306
  1019.2 106.5 %all-gather.33.cloned.1.call-start = ((), (), s32[]{:S(2)}) async-start(), calls=%async_computation.12 | async-start | bytes 2621440 | tf_op jit(solution)/shard_map/all_gather | solution.py:234
  1022.1 140.6 %all-gather.43.cloned.1.call-start = ((), (), s32[]{:S(2)}) async-start(), calls=%async_computation.18 | async-start | bytes 2621440 | tf_op jit(solution)/shard_map/all_gather | solution.py:307
  1029.8 6.4 collective-permute-start.2
  1031.2 194.4 %reduce-scatter.6.cloned.1.call-start = ((), (), s32[]{:S(2)}) async-start(), calls=%async_computation.19 | async-start | bytes 5242880 | tf_op jit(solution)/shard_map/reduce_scatter | solution.py:324
  1172.7 233.4 %all-reduce.16.cloned.1.call-start = ((), (), s32[]{:S(2)}) async-start(), calls=%async_computation.25 | async-start | bytes 8388608 | tf_op jit(solution)/shard_map/psum | solution.py:348
  1250.6 194.2 %all-gather.45.cloned.1.call-start = ((), (), s32[]{:S(2)}) async-start(), calls=%async_computation.20 | async-start | bytes 2621440 | tf_op jit(solution)/shard_map/all_gather | solution.py:306
  1251.2 228.1 %all-gather.47.cloned.1.call-start = ((), (), s32[]{:S(2)}) async-start(), calls=%async_computation.21 | async-start | bytes 2621440 | tf_op jit(solution)/shard_map/all_gather | solution.py:307
  1418.3 31.0 %collective-permute-start.3 = (bf16[2,256,2048]{2,1,0:T(8,128)(2,1)}, bf16[2,256,2048]{2,1,0:T(8,128)(2,1)}, u32[]{:S(2)}, u32[]{:S(2)}) collective-permute-start(bf16[2,256,2048]{2,1,0:T(8,128)(2,1)} %bitcast.58), channel_id=1, source_target_pairs={{16,0},{17,1},{18,2},{19,3},{20,4},{21,5},{22,6},{23,7},{24,8},{25... | collective-permute-start | bytes 6291464 | tf_op jit(solution)/shard_map/ppermute | solution.py:16
  1434.3 120.2 %reduce-scatter.8.cloned.1.call-start = ((), (), s32[]{:S(2)}) async-start(), calls=%async_computation.22 | async-start | bytes 5242880 | tf_op jit(solution)/shard_map/reduce_scatter | solution.py:324
  1489.3 309.3 %all-reduce.14.cloned.1.call-start = ((), (), s32[]{:S(2)}) async-start(), calls=%async_computation.24 | async-start | bytes 12582912 | tf_op jit(solution)/shard_map/psum | solution.py:249
  1574.4 739.3 %all-reduce.12.cloned.1.call-start = ((), (), s32[]{:S(2)}) async-start(), calls=%async_computation.23 | async-start | bytes 50386944
  (166 other events, 5931.9 us)
Sparse Core Ops, SparseCore 0:
  9.9 74.4 all-gather.16
  104.2 35.4 all-gather.20
  142.1 35.2 all-gather.18
  179.1 87.5 all-gather.24
  268.5 87.4 all-gather.26
  357.6 35.1 all-gather.22
  398.4 86.5 all-reduce.9
  518.6 35.1 all-gather.30
  556.3 35.2 all-gather.36
  593.5 35.2 all-gather.28
  630.8 35.2 all-gather.38
  676.3 52.6 reduce-scatter.3
  753.8 223.5 all-reduce.17
  1017.1 34.3 all-gather.34
  1053.3 35.2 all-gather.40
  1090.3 35.2 all-gather.32
  1127.4 35.2 all-gather.42
  1172.8 52.6 reduce-scatter.5
  1250.7 155.3 all-reduce.15
  1407.8 34.3 all-gather.44
  1444.0 35.2 all-gather.46
  1489.5 52.6 reduce-scatter.7
  1574.5 224.1 all-reduce.13
  1871.0 442.6 all-reduce.11
where the time goes:
time: 2460 us; the launch traced here: 2450 us
  waiting for transfers between devices  1560 us (63%)
  matrix products  336 us (14%)
  local copies, waits for them, and re-layouts  309 us (13%)
  other arithmetic  161 us (7%)
  blocking collectives  59.8 us (2%)
    psum x3, waiting for transfers between devices, on_device(): lax.psum(partial_sum.astype(jnp.bfloat16), 'tp').astype(jnp.float32)  445 us
    unnamed x25, waiting for transfers between devices  432 us
    psum x1, waiting for transfers between devices, on_device(): lax.psum(back_two.astype(jnp.bfloat16), 'tp').astype(jnp.float32)  155 us
    dot_general x12, matrix products, transposed_dot(): lax.dot_general(left, right, (((0,), (0,)), ((), ())), preferred_element_...  107 us
    slice x5, local copies, waits for them, and re-layouts, unpack_terms(): packed[:, offset:offset + span_size]  93.8 us
    all_gather x3, waiting for transfers between devices, on_device(): lax.all_gather(layer_value_rows, 'ctx', axis=1, tiled=True)  91.6 us
    dot_general x12, matrix products, dot_transposed(): lax.dot_general(left, right, (((1,), (1,)), ((), ())), preferred_element_...  84.4 us
    all_gather x1, waiting for transfers between devices, on_device(): lax.all_gather(w_up, 'ctx', axis=1, tiled=True)  84.1 us
  transfers between devices with their start and end apart: 28, of which 25 were waited for; matrix products, arithmetic and copies ran while one was open for 16% of the time, Pallas kernels for 0%

commit v1 on v0

v1 whole, which is shorter than its diff:
```python
import math

import jax
import jax.numpy as jnp
from jax import lax
from jax.sharding import PartitionSpec as P

norm_eps = 1e-05
root_half = 1.0 / math.sqrt(2.0)
root_tau = 1.0 / math.sqrt(2.0 * math.pi)


def one_way(value, src, dst):
    return lax.ppermute(value, "section", [(src, dst)])


def swap_sections(value):
    return lax.ppermute(value, "section", [(0, 1), (1, 0)])


def gelu_parts(values):
    normal_cdf = 0.5 * (1.0 + lax.erf(values * root_half))
    return (values * normal_cdf, normal_cdf + values * jnp.exp(-0.5 * values * values) * root_tau)


def rotary_tables(positions, rot_width):
    half_width = rot_width // 2
    frequency = jnp.exp(
        jnp.arange(half_width).astype(jnp.float32) * (-2.0 * math.log(10000.0) / rot_width)
    )
    angles = positions[:, None] * frequency[None, :]
    cosine = jnp.cos(angles)
    sine = jnp.sin(angles)
    return (
        jnp.concatenate([cosine, cosine], -1)[:, None, :],
        jnp.concatenate([sine, sine], -1)[:, None, :],
    )


def rotate_heads(features, cosine, sine):
    rot_width = cosine.shape[-1]
    half_width = rot_width // 2
    rotated_part = features[..., :rot_width]
    turned = jnp.concatenate([-rotated_part[..., half_width:], rotated_part[..., :half_width]], -1)
    return jnp.concatenate([rotated_part * cosine + turned * sine, features[..., rot_width:]], -1)


def rotate_back(grads, cosine, sine):
    rot_width = cosine.shape[-1]
    half_width = rot_width // 2
    rotated_part = grads[..., :rot_width]
    weighted = rotated_part * sine
    turned = jnp.concatenate([weighted[..., half_width:], -weighted[..., :half_width]], -1)
    return jnp.concatenate([rotated_part * cosine + turned, grads[..., rot_width:]], -1)


def dot_transposed(left, right):
    return lax.dot_general(
        left, right, (((1,), (1,)), ((), ())), preferred_element_type=jnp.float32
    )


def transposed_dot(left, right):
    return lax.dot_general(
        left, right, (((0,), (0,)), ((), ())), preferred_element_type=jnp.float32
    )


def masked_scores(query_rows, key_all, allowed, score_scale):
    scores = (
        jnp.einsum("sqhd,skhd->shqk", query_rows, key_all, preferred_element_type=jnp.float32)
        * score_scale
    )
    return jnp.where(allowed, scores, -1e30)


def attend_heads(query_rows, key_all, value_all, allowed, score_scale):
    scores = masked_scores(query_rows, key_all, allowed, score_scale)
    row_top = jnp.max(scores, axis=-1, keepdims=True)
    row_total = jnp.sum(jnp.exp(scores - row_top), axis=-1, keepdims=True)
    log_total = row_top + jnp.log(row_total)
    probabilities = jnp.where(allowed, jnp.exp(scores - log_total), 0.0)
    context = jnp.einsum(
        "shqk,skhd->sqhd",
        probabilities.astype(jnp.bfloat16),
        value_all,
        preferred_element_type=jnp.float32,
    ).astype(jnp.bfloat16)
    return (context, log_total)


def attend_back(
    query_rows, key_all, value_all, context, log_total, grad_context, allowed, score_scale
):
    scores = masked_scores(query_rows, key_all, allowed, score_scale)
    probabilities = jnp.where(allowed, jnp.exp(scores - log_total), 0.0)
    grad_half = grad_context.astype(jnp.bfloat16)
    row_delta = jnp.sum(grad_context * context.astype(jnp.float32), axis=-1).transpose(0, 2, 1)[
        ..., None
    ]
    grad_probs = jnp.einsum(
        "sqhd,skhd->shqk", grad_half, value_all, preferred_element_type=jnp.float32
    )
    grad_scores = (probabilities * (grad_probs - row_delta)).astype(jnp.bfloat16)
    grad_query = (
        jnp.einsum("shqk,skhd->sqhd", grad_scores, key_all, preferred_element_type=jnp.float32)
        * score_scale
    )
    grad_key = (
        jnp.einsum("shqk,sqhd->skhd", grad_scores, query_rows, preferred_element_type=jnp.float32)
        * score_scale
    )
    grad_value = jnp.einsum(
        "shqk,sqhd->skhd",
        probabilities.astype(jnp.bfloat16),
        grad_half,
        preferred_element_type=jnp.float32,
    )
    return (grad_query, grad_key, grad_value)


def gather_layer(ln1_gain, ln1_bias, ln2_gain, ln2_bias, w_qkv, qkv_bias, w_dense, w_up,
                 up_bias, w_down, out_bias):
    gains = lax.all_gather(
        jnp.concatenate([ln1_gain, ln1_bias, ln2_gain, ln2_bias, out_bias], 0),
        "ctx", axis=1, tiled=True,
    )
    return (
        gains,
        lax.all_gather(up_bias[0], "ctx", axis=0, tiled=True),
        lax.all_gather(w_qkv[0], "ctx", axis=0, tiled=True),
        lax.all_gather(qkv_bias[0], "ctx", axis=1, tiled=True),
        lax.all_gather(w_dense[0], "ctx", axis=1, tiled=True),
        lax.all_gather(w_up[0], "ctx", axis=0, tiled=True),
        lax.all_gather(w_down[0], "ctx", axis=1, tiled=True),
    )


def layer_forward(rows, weights, cosine, sine, allowed, score_scale):
    gains, up_shift, qkv_full, qkv_shift, dense_full, up_full, down_full = weights
    seq_count, tok_rows, model_width = rows.shape
    head_count = qkv_full.shape[1]
    head_dim = qkv_full.shape[2] // 3
    flat_count = seq_count * tok_rows
    gain_one, bias_one, gain_two, bias_two, out_shift = (
        gains[i].astype(jnp.float32) for i in range(5)
    )
    up_shift = up_shift.astype(jnp.float32)
    flat_rows = rows.reshape(flat_count, model_width).astype(jnp.float32)
    row_mean = jnp.mean(flat_rows, axis=-1, keepdims=True)
    centered = flat_rows - row_mean
    row_var = jnp.mean(centered * centered, axis=-1, keepdims=True)
    inverse = lax.rsqrt(row_var + norm_eps)
    unit = centered * inverse
    input_one = (unit * gain_one + bias_one).astype(jnp.bfloat16)
    input_two = (unit * gain_two + bias_two).astype(jnp.bfloat16)
    mixed_rows = jnp.dot(
        input_one, qkv_full.reshape(model_width, -1), preferred_element_type=jnp.float32
    ) + qkv_shift.astype(jnp.float32).reshape(-1)
    mixed_rows = mixed_rows.reshape(seq_count, tok_rows, head_count, 3 * head_dim)
    query_rows = rotate_heads(mixed_rows[..., :head_dim], cosine, sine).astype(jnp.bfloat16)
    key_rows = rotate_heads(mixed_rows[..., head_dim : 2 * head_dim], cosine, sine).astype(
        jnp.bfloat16
    )
    value_rows = mixed_rows[..., 2 * head_dim :].astype(jnp.bfloat16)
    key_all = lax.all_gather(key_rows, "ctx", axis=1, tiled=True)
    value_all = lax.all_gather(value_rows, "ctx", axis=1, tiled=True)
    context, log_total = attend_heads(query_rows, key_all, value_all, allowed, score_scale)
    pre_act = jnp.dot(input_two, up_full, preferred_element_type=jnp.float32) + up_shift
    activated, slope = gelu_parts(pre_act)
    active = activated.astype(jnp.bfloat16)
    partial_sum = jnp.dot(
        context.reshape(flat_count, -1), dense_full, preferred_element_type=jnp.float32
    )
    partial_sum = partial_sum + jnp.dot(active, down_full, preferred_element_type=jnp.float32)
    branch = lax.psum(partial_sum.astype(jnp.bfloat16), "tp").astype(jnp.float32)
    result = (flat_rows + branch + out_shift).reshape(seq_count, tok_rows, model_width)
    saved = (unit, inverse, input_one, input_two, query_rows, key_all, value_all, context,
             log_total, slope, active)
    return result, saved


def layer_backward(grad_rows, saved, weights, cosine, sine, allowed, score_scale):
    gains, _, qkv_full, qkv_shift, dense_full, up_full, down_full = weights
    (unit, inverse, input_one, input_two, query_rows, key_all, value_all, context, log_total,
     slope, active) = saved
    seq_count, tok_rows, model_width = grad_rows.shape
    head_count = qkv_full.shape[1]
    head_dim = qkv_full.shape[2] // 3
    flat_count = seq_count * tok_rows
    gain_one = gains[0].astype(jnp.float32)
    gain_two = gains[2].astype(jnp.float32)
    grad_flat = grad_rows.reshape(flat_count, model_width)
    grad_half = grad_flat.astype(jnp.bfloat16)
    grad_out_shift = jnp.sum(grad_flat, 0)
    grad_down = transposed_dot(active, grad_half)
    grad_pre = dot_transposed(grad_half, down_full) * slope
    grad_up_shift = jnp.sum(grad_pre, 0)
    pre_half = grad_pre.astype(jnp.bfloat16)
    grad_up = transposed_dot(input_two, pre_half)
    back_two = dot_transposed(pre_half, up_full)
    grad_dense = transposed_dot(context.reshape(flat_count, -1), grad_half)
    grad_context = dot_transposed(grad_half, dense_full).reshape(
        seq_count, tok_rows, head_count, head_dim
    )
    grad_query, grad_key_all, grad_value_all = attend_back(
        query_rows, key_all, value_all, context, log_total, grad_context, allowed, score_scale
    )
    key_value_grads = lax.psum_scatter(
        jnp.stack([grad_key_all, grad_value_all]).astype(jnp.bfloat16),
        "ctx",
        scatter_dimension=2,
        tiled=True,
    ).astype(jnp.float32)
    grad_mixed = jnp.concatenate(
        [
            rotate_back(grad_query, cosine, sine),
            rotate_back(key_value_grads[0], cosine, sine),
            key_value_grads[1],
        ],
        -1,
    )
    grad_qkv_shift = jnp.sum(grad_mixed, (0, 1))
    mixed_half = grad_mixed.reshape(flat_count, -1).astype(jnp.bfloat16)
    grad_qkv = transposed_dot(input_one, mixed_half).reshape(qkv_full.shape)
    back_one = dot_transposed(mixed_half, qkv_full.reshape(model_width, -1))
    norm_terms = jnp.stack(
        [
            jnp.sum(back_one * unit, 0),
            jnp.sum(back_one, 0),
            jnp.sum(back_two * unit, 0),
            jnp.sum(back_two, 0),
        ]
    )
    scaled = lax.psum(
        (back_one * gain_one + back_two * gain_two).astype(jnp.bfloat16), "tp"
    ).astype(jnp.float32)
    first_mean = jnp.mean(scaled, axis=-1, keepdims=True)
    second_mean = jnp.mean(scaled * unit, axis=-1, keepdims=True)
    grad_input = grad_flat + inverse * (scaled - first_mean - unit * second_mean)
    small = jnp.concatenate(
        [norm_terms, grad_out_shift[None]], 0
    )
    grad_terms = (small, grad_qkv, grad_qkv_shift, grad_dense, grad_up, grad_up_shift, grad_down)
    return grad_input.reshape(seq_count, tok_rows, model_width), grad_terms


def on_device(
    inputs,
    grad_out,
    ln1_gain,
    ln1_bias,
    ln2_gain,
    ln2_bias,
    w_qkv,
    qkv_bias,
    w_dense,
    w_up,
    up_bias,
    w_down,
    out_bias,
):
    section_index = lax.axis_index("section")
    context_index = lax.axis_index("ctx")
    ctx_count = lax.axis_size("ctx")
    micro_count, seq_count, tok_rows, model_width = inputs.shape
    seq_length = tok_rows * ctx_count
    head_dim = w_qkv.shape[3] // 3
    score_scale = 1.0 / math.sqrt(head_dim)

    own = gather_layer(ln1_gain, ln1_bias, ln2_gain, ln2_bias, w_qkv, qkv_bias, w_dense, w_up,
                       up_bias, w_down, out_bias)
    other = tuple(swap_sections(piece) for piece in own)
    first_layer = tuple(jnp.where(section_index == 0, a, b) for a, b in zip(own, other))
    second_layer = tuple(jnp.where(section_index == 0, b, a) for a, b in zip(own, other))

    query_index = context_index * tok_rows + jnp.arange(tok_rows, dtype=jnp.int32)
    allowed = jnp.arange(seq_length, dtype=jnp.int32)[None, :] <= query_index[:, None]
    cosine, sine = rotary_tables(query_index.astype(jnp.float32), head_dim // 4)

    rows = jnp.where(section_index == 0, inputs[0], inputs[1])
    grads = jnp.where(section_index == 0, grad_out[0], grad_out[1])

    mid, saved_first = layer_forward(rows, first_layer, cosine, sine, allowed, score_scale)
    top, saved_second = layer_forward(
        mid.astype(jnp.bfloat16), second_layer, cosine, sine, allowed, score_scale
    )
    top_other = one_way(top, 0, 1)

    grad_mid, terms_second = layer_backward(
        grads, saved_second, second_layer, cosine, sine, allowed, score_scale
    )
    second_other = tuple(one_way(t.astype(jnp.bfloat16), 0, 1) for t in terms_second)
    grad_in, terms_first = layer_backward(
        grad_mid, saved_first, first_layer, cosine, sine, allowed, score_scale
    )
    first_other = tuple(one_way(t.astype(jnp.bfloat16), 1, 0) for t in terms_first)
    grad_other = one_way(grad_in, 1, 0)

    totals = tuple(
        jnp.where(
            section_index == 0,
            a + b.astype(jnp.float32),
            c + d.astype(jnp.float32),
        )
        for a, b, c, d in zip(terms_first, first_other, terms_second, second_other)
    )
    small, g_qkv, g_qkv_shift, g_dense, g_up, g_up_shift, g_down = totals
    small = lax.psum(small[:4], "tp")
    small = jnp.concatenate([small, totals[0][4:]], 0)

    def scatter(value, axis):
        return lax.psum_scatter(
            value.astype(jnp.bfloat16), "ctx", scatter_dimension=axis, tiled=True
        ).astype(jnp.float32)

    small = scatter(small, 1)
    g_qkv = scatter(g_qkv, 0)
    g_qkv_shift = scatter(g_qkv_shift, 1)
    g_dense = scatter(g_dense, 1)
    g_up = scatter(g_up, 0)
    g_up_shift = scatter(g_up_shift, 0)
    g_down = scatter(g_down, 1)

    block_ends = jnp.where(
        section_index == 0,
        jnp.stack([grad_in, grad_other]),
        jnp.stack([top_other, top]),
    )[None]
    return (
        block_ends,
        small[0][None],
        small[1][None],
        small[2][None],
        small[3][None],
        g_qkv[None],
        g_qkv_shift[None],
        g_dense[None],
        g_up[None],
        g_up_shift[None],
        g_down[None],
        small[4][None],
    )


def solution(mesh):
    placed = (
        P(None, None, "ctx", None),
        P(None, None, "ctx", None),
        P("section", "ctx"),
        P("section", "ctx"),
        P("section", "ctx"),
        P("section", "ctx"),
        P("section", "ctx", "tp", None),
        P("section", "tp", "ctx"),
        P("section", "tp", "ctx"),
        P("section", "ctx", "tp"),
        P("section", ("tp", "ctx")),
        P("section", "tp", "ctx"),
        P("section", "ctx"),
    )
    return jax.shard_map(
        on_device,
        mesh=mesh,
        in_specs=placed,
        out_specs=(
            P("section", None, None, "ctx", None),
            P("section", "ctx"),
            P("section", "ctx"),
            P("section", "ctx"),
            P("section", "ctx"),
            P("section", "ctx", "tp", None),
            P("section", "tp", "ctx"),
            P("section", "tp", "ctx"),
            P("section", "ctx", "tp"),
            P("section", ("tp", "ctx")),
            P("section", "tp", "ctx"),
            P("section", "ctx"),
        ),
        check_vma=False,
    )
```

time: 2460 us -> 1410 us (0.57)
  waiting for transfers between devices: 1560 us -> 817 us
  local copies, waits for them, and re-layouts: 309 us -> 98.2 us
  matrix products: 336 us -> 216 us
  starting transfers between devices: 10.2 us -> 47.9 us
    unnamed x25 -> x20, waiting for transfers between devices: 432 us -> 1.66 us
    psum x4 -> x3, waiting for transfers between devices: 600 us -> 287 us  [the longest x2 202 us: layer_backward(): lax.psum((back_one * gain_one + back_two * gain_two).astype(jnp.bfloat16)...]
    all_gather x16 -> x8, waiting for transfers between devices: 480 us -> 334 us  [the longest x1 89.5 us: gather_layer(): lax.all_gather(w_up[0], 'ctx', axis=0, tiled=True)]
    reduce_scatter x3 -> x7, waiting for transfers between devices: 35.2 us -> 161 us  [the longest x5 132 us: scatter(): lax.psum_scatter(value.astype(jnp.bfloat16), 'ctx', scatter_dimension=axi...]
    slice x6 -> x5, local copies, waits for them, and re-layouts: 95.7 us -> 5.24 us  [the longest x2 3.74 us: layer_forward(): value_rows = mixed_rows[..., 2 * head_dim:].astype(jnp.bfloat16)]
    reshape x19 -> x8, local copies, waits for them, and re-layouts: 73.5 us -> 18.5 us  [the longest x6 15.3 us: layer_forward(): mixed_rows.reshape(seq_count, tok_rows, head_count, 3 * head_dim)]
    unnamed x369 -> x184, local copies, waits for them, and re-layouts: 69.1 us -> 27.8 us
    ppermute x4 -> x23, starting transfers between devices: 7.86 us -> 45.9 us  [the longest x16 45.6 us: one_way(): return lax.ppermute(value, 'section', [(src, dst)])]
  transfers between devices with their start and end apart: 28 -> 42, of which waited for: 25 -> 20; matrix products, arithmetic and copies ran while one was open for 16% -> 25% of each run, Pallas kernels for 0% -> 0%
where the time goes in v1:
time: 1410 us; the launch traced here: 1400 us
  waiting for transfers between devices  817 us (58%)
  matrix products  216 us (15%)
  other arithmetic  155 us (11%)
  local copies, waits for them, and re-layouts  98.2 us (7%)
  blocking collectives  52.8 us (4%)
  starting transfers between devices  47.9 us (3%)
  between operations  16.6 us (1%)
    psum x2, waiting for transfers between devices, layer_backward(): lax.psum((back_one * gain_one + back_two * gain_two).astype(jnp.bfloat16)...  202 us
    reduce_scatter x5, waiting for transfers between devices, scatter(): lax.psum_scatter(value.astype(jnp.bfloat16), 'ctx', scatter_dimension=axi...  132 us
    all_gather x1, waiting for transfers between devices, gather_layer(): lax.all_gather(w_up[0], 'ctx', axis=0, tiled=True)  89.5 us
    psum x1, waiting for transfers between devices, layer_forward(): lax.psum(partial_sum.astype(jnp.bfloat16), 'tp').astype(jnp.float32)  85 us
    all_gather x1, waiting for transfers between devices, gather_layer(): lax.all_gather(w_qkv[0], 'ctx', axis=0, tiled=True)  71.8 us
    dot_general x8, matrix products, transposed_dot(): lax.dot_general(left, right, (((0,), (0,)), ((), ())), preferred_element_...  68.6 us
    dot_general x8, matrix products, dot_transposed(): lax.dot_general(left, right, (((1,), (1,)), ((), ())), preferred_element_...  67.1 us
    all_gather x2, waiting for transfers between devices, layer_forward(): value_all = lax.all_gather(value_rows, 'ctx', axis=1, tiled=True)  65.5 us
  transfers between devices with their start and end apart: 42, of which 20 were waited for; matrix products, arithmetic and copies ran while one was open for 25% of the time, Pallas kernels for 0%

profile of v1, /device:TPU:0, one launch (start us, length us, event | category | flops | bytes accessed | tf_op | source)
XLA Modules:
  0.0 1403.4 jit_solution(14011141501607552604)
XLA Ops:
  11.6 71.8 %all-gather.23.cloned.1.call-done = bf16[1,2048,2,768]{3,1,2,0:T(8,128)(2,1)} async-done(((bf16[1,512,2,768]{3,1,2,0:T(8,128)(2,1)}), bf16[1,2048,2,768]{3,1,2,0:T(8,128)(2,1)}) %all-gather.23.cloned.1.call-update) | async-done | bytes 6291472 | tf_op jit(solution)/shard_map/all_gather | solution.py:131
  83.6 9.6 all-gather.1
  108.3 64.7 %all-gather.29.cloned.1.call-done = bf16[1,2048,2048]{2,1,0:T(8,128)(2,1)} async-done(((bf16[1,2048,512]{2,1,0:T(8,128)(2,1)}), bf16[1,2048,2048]{2,1,0:T(8,128)(2,1)}) %all-gather.29.cloned.1.call-update) | async-done | bytes 8388624 | tf_op jit(solution)/shard_map/all_gather | solution.py:135
  173.0 89.5 %all-gather.27.cloned.1.call-done = bf16[1,2048,2048]{2,1,0:T(8,128)(2,1)} async-done(((bf16[1,512,2048]{2,1,0:T(8,128)(2,1)}), bf16[1,2048,2048]{2,1,0:T(8,128)(2,1)}) %all-gather.27.cloned.1.call-update) | async-done | bytes 8388624 | tf_op jit(solution)/shard_map/all_gather | solution.py:134
  262.5 10.3 broadcast_select_fusion.5
  315.2 21.8 %all-gather.17.cloned.1.call-done = bf16[2,1024,2,256]{3,1,2,0:T(8,128)(2,1)} async-done(((bf16[2,256,2,256]{3,1,2,0:T(8,128)(2,1)}), bf16[2,1024,2,256]{3,1,2,0:T(8,128)(2,1)}) %all-gather.17.cloned.1.call-update) | async-done | bytes 2097168 | tf_op jit(solution)/shard_map/all_gather | solution.py:166
  341.6 33.0 %all-gather.15.cloned.1.call-done = bf16[2,1024,2,256]{3,1,2,0:T(8,128)(2,1)} async-done(((bf16[2,256,2,256]{3,1,2,0:T(8,128)(2,1)}), bf16[2,1024,2,256]{3,1,2,0:T(8,128)(2,1)}) %all-gather.15.cloned.1.call-update) | async-done | bytes 2097168 | tf_op jit(solution)/shard_map/all_gather | solution.py:167
  405.0 85.0 %all-reduce.6.cloned.1.call-done = bf16[512,2048]{1,0:T(8,128)(2,1)} async-done(((bf16[512,2048]{1,0:T(8,128)(2,1)}), bf16[512,2048]{1,0:T(8,128)(2,1)}) %all-reduce.6.cloned.1.call-update) | async-done | bytes 2097168 | tf_op jit(solution)/shard_map/psum | solution.py:176
  524.3 20.5 %all-gather.19.cloned.1.call-done = bf16[2,1024,2,256]{3,1,2,0:T(8,128)(2,1)} async-done(((bf16[2,256,2,256]{3,1,2,0:T(8,128)(2,1)}), bf16[2,1024,2,256]{3,1,2,0:T(8,128)(2,1)}) %all-gather.19.cloned.1.call-update) | async-done | bytes 2097168 | tf_op jit(solution)/shard_map/all_gather | solution.py:166
  550.2 32.5 %all-gather.21.cloned.1.call-done = bf16[2,1024,2,256]{3,1,2,0:T(8,128)(2,1)} async-done(((bf16[2,256,2,256]{3,1,2,0:T(8,128)(2,1)}), bf16[2,1024,2,256]{3,1,2,0:T(8,128)(2,1)}) %all-gather.21.cloned.1.call-update) | async-done | bytes 2097168 | tf_op jit(solution)/shard_map/all_gather | solution.py:167
  606.3 13.0 fusion.141
  621.5 28.6 %reduce-scatter.11.cloned.1.call-done = bf16[2,2,256,2,256]{4,2,3,1,0:T(8,128)(2,1)} async-done(((bf16[2,2,1024,2,256]{4,2,3,1,0:T(8,128)(2,1)}), bf16[2,2,256,2,256]{4,2,3,1,0:T(8,128)(2,1)}) %reduce-scatter.11.cloned.1.call-update) | async-done | bytes 1048592 | tf_op jit(solution)/shard_map/reduce_scatter | solution.py:209
  671.7 14.6 %fusion.120 = (f32[2048]{0:T(1024)S(1)}, f32[2048]{0:T(1024)S(1)}, bf16[512,2048]{1,0:T(8,128)(2,1)}) fusion(f32[512]{0:T(512)S(1)} %add_rsqrt_fusion, f32[512]{0:T(512)S(1)} %broadcast_multiply_fusion.4, bf16[512,2048]{1,0:T(8,128)(2,1)S(1)} %get-tuple-element.79, f32[2048]{0:T(1024)S(1)} %bitcast.290, f32[512,2048]{1,0:T(8,128)S(1)} %fusion.145, ...), kind=kOutput, calls=%fused_computation.251 | convolution fusion | flops 4309643264 | bytes 27299840 | tf_op jit(solution)/shard_map/dot_general | solution.py:58
  686.4 86.6 %all-reduce.8.cloned.1.call-done = bf16[512,2048]{1,0:T(8,128)(2,1)} async-done(((bf16[512,2048]{1,0:T(8,128)(2,1)}), bf16[512,2048]{1,0:T(8,128)(2,1)}) %all-reduce.8.cloned.1.call-update) | async-done | bytes 2097168 | tf_op jit(solution)/shard_map/psum | solution.py:235
  802.4 13.0 fusion.139
  822.7 12.7 fusion.55
  845.7 9.7 fusion.142
  879.7 11.2 fusion.118
  891.0 15.7 %fusion.140 = (bf16[2048,2048]{1,0:T(8,128)(2,1)}, f32[2048,2048]{1,0:T(8,128)}) fusion(bf16[512,2048]{1,0:T(8,128)(2,1)} %fusion.45, bf16[512,2048]{1,0:T(8,128)(2,1)} %get-tuple-element.176), kind=kOutput, calls=%fused_computation.269 | convolution fusion | flops 4299161600 | bytes 29360128 | tf_op jit(solution)/shard_map/dot_general | solution.py:64
  933.1 115.2 %all-reduce.10.cloned.1.call-done = (bf16[512,2048]{1,0:T(8,128)(2,1)}, bf16[512,2048]{1,0:T(8,128)(2,1)}) async-done(((bf16[512,2048]{1,0:T(8,128)(2,1)}, bf16[512,2048]{1,0:T(8,128)(2,1)}), (bf16[512,2048]{1,0:T(8,128)(2,1)}, bf16[512,2048]{1,0:T(8,128)(2,1)})) %all-reduce.10.cloned.1.call-update) | async-done | bytes 4194320 | tf_op jit(solution)/shard_map/psum | solution.py:235
  1055.9 16.8 %psum.39 = bf16[4,2048]{1,0:T(4,128)(2,1)S(1)} all-reduce(f32[4,2048]{1,0:T(4,128)S(1)} %slice.315), channel_id=1, replica_groups=mesh['section'=2,'ctx'=4,'tp'=4] {'tp'}, use_global_device_ids=true, to_apply=%region_30.31 | all-reduce | flops 8192 | bytes 49152 | tf_op jit(solution)/shard_map/psum | solution.py:309
  1073.5 21.0 %select_convert_fusion.1 = bf16[2048,2048]{1,0:T(8,128)(2,1)} fusion(f32[2048,2048]{1,0:T(8,128)} %get-tuple-element.170, bf16[2048,2048]{1,0:T(8,128)(2,1)} %collective-permute-done.18, f32[2048,2048]{1,0:T(8,128)} %get-tuple-element.172, bf16[2048,2048]{1,0:T(8,128)(2,1)} %collective-permute-done.17, pred[]{:T(512)S(6)} %eq.2), kind=kLoop, calls=%fused_computation.1 | loop fusion | flops 25165824 | bytes 58720256 | tf_op jit(solution)/shard_map/convert_element_type | solution.py:314
  1108.5 12.3 fusion.144
  1122.1 14.1 %collective-permute-done.21 = bf16[2048,2048]{1,0:T(8,128)(2,1)} collective-permute-done((bf16[2048,2048]{1,0:T(8,128)(2,1)}, bf16[2048,2048]{1,0:T(8,128)(2,1)}, u32[]{:S(2)}, u32[]{:S(2)}) %collective-permute-start.21) | collective-permute-done | bytes 8388640 | tf_op jit(solution)/shard_map/ppermute | solution.py:14
  1136.2 15.7 %select_convert_fusion = bf16[2048,2048]{1,0:T(8,128)(2,1)} fusion(f32[2048,2048]{1,0:T(8,128)S(1)} %get-tuple-element.178, bf16[2048,2048]{1,0:T(8,128)(2,1)} %collective-permute-done.22, f32[2048,2048]{1,0:T(8,128)} %get-tuple-element.180, bf16[2048,2048]{1,0:T(8,128)(2,1)} %collective-permute-done.21, pred[]{:T(512)S(6)} %eq.2), kind=kLoop, calls=%fused_computation | loop fusion | flops 25165824 | bytes 58720256 | tf_op jit(solution)/shard_map/convert_element_type | solution.py:314
  1155.0 10.1 fusion.135
  1179.0 10.7 collective-permute-done.11
  1189.8 11.4 select_convert_fusion.2
  1223.3 10.5 all-reduce
  1239.6 10.6 maximum_select_fusion
  1254.3 63.1 %reduce-scatter.23.cloned.1.call-done = bf16[2048,512]{1,0:T(8,128)(2,1)} async-done(((bf16[2048,2048]{1,0:T(8,128)(2,1)}), bf16[2048,512]{1,0:T(8,128)(2,1)}) %reduce-scatter.23.cloned.1.call-update) | async-done | bytes 2097168 | tf_op jit(solution)/shard_map/reduce_scatter | solution.py:313
  1321.7 69.3 %reduce-scatter.17.cloned.1.call-done = bf16[512,2,768]{2,0,1:T(8,128)(2,1)} async-done(((bf16[2048,2,768]{2,0,1:T(8,128)(2,1)}), bf16[512,2,768]{2,0,1:T(8,128)(2,1)}) %reduce-scatter.17.cloned.1.call-update) | async-done | bytes 1572880 | tf_op jit(solution)/shard_map/reduce_scatter | solution.py:313
  (417 shorter events, 362.1 us)
Async XLA Ops:
  7.2 76.1 %all-gather.23.cloned.1.call-start = ((), (), s32[]{:S(2)}) async-start(), calls=%async_computation.21 | async-start | bytes 7864320 | tf_op jit(solution)/shard_map/all_gather | solution.py:131
  10.1 162.9 %all-gather.29.cloned.1.call-start = ((), (), s32[]{:S(2)}) async-start(), calls=%async_computation.24 | async-start | bytes 10485760 | tf_op jit(solution)/shard_map/all_gather | solution.py:135
  10.8 251.7 %all-gather.27.cloned.1.call-start = ((), (), s32[]{:S(2)}) async-start(), calls=%async_computation.23 | async-start | bytes 10485760 | tf_op jit(solution)/shard_map/all_gather | solution.py:134
  11.5 303.5 %all-gather.25.cloned.1.call-start = ((), (), s32[]{:S(2)}) async-start(), calls=%async_computation.22 | async-start | bytes 2621440 | tf_op jit(solution)/shard_map/all_gather | solution.py:133
  83.4 179.1 %collective-permute-start.1 = (bf16[2048,2,768]{2,0,1:T(8,128)(2,1)}, bf16[2048,2,768]{2,0,1:T(8,128)(2,1)}, u32[]{:S(2)}, u32[]{:S(2)}) collective-permute-start(bf16[2048,2,768]{2,0,1:T(8,128)(2,1)} %bitcast.281), channel_id=1, source_target_pairs={{0,16},{16,0},{1,17},{17,1},{2,18},{18,2},{3,19},{19,3},{4,20},{20... | collective-permute-start | bytes 18874376 | tf_op jit(solution)/shard_map/ppermute | solution.py:18
  101.0 236.0 %all-gather.17.cloned.1.call-start = ((), (), s32[]{:S(2)}) async-start(), calls=%async_computation.9 | async-start | bytes 2621440 | tf_op jit(solution)/shard_map/all_gather | solution.py:166
  173.0 215.8 %collective-permute-start.6 = (bf16[2048,2048]{1,0:T(8,128)(2,1)}, bf16[2048,2048]{1,0:T(8,128)(2,1)}, u32[]{:S(2)}, u32[]{:S(2)}) collective-permute-start(bf16[2048,2048]{1,0:T(8,128)(2,1)} %bitcast.328), channel_id=1, source_target_pairs={{0,16},{16,0},{1,17},{17,1},{2,18},{18,2},{3,19},{19,3},{4,20},{20... | collective-permute-start | bytes 25165832 | tf_op jit(solution)/shard_map/ppermute | solution.py:18
  262.5 119.0 %collective-permute-start.4 = (bf16[2048,2048]{1,0:T(8,128)(2,1)}, bf16[2048,2048]{1,0:T(8,128)(2,1)}, u32[]{:S(2)}, u32[]{:S(2)}) collective-permute-start(bf16[2048,2048]{1,0:T(8,128)(2,1)} %bitcast.327), channel_id=1, source_target_pairs={{0,16},{16,0},{1,17},{17,1},{2,18},{18,2},{3,19},{19,3},{4,20},{20... | collective-permute-start | bytes 25165832 | tf_op jit(solution)/shard_map/ppermute | solution.py:18
  301.1 73.5 %all-gather.15.cloned.1.call-start = ((), (), s32[]{:S(2)}) async-start(), calls=%async_computation.8 | async-start | bytes 2621440 | tf_op jit(solution)/shard_map/all_gather | solution.py:167
  303.0 187.0 %all-reduce.6.cloned.1.call-start = ((), (), s32[]{:S(2)}) async-start(), calls=%async_computation.10 | async-start | bytes 4194304 | tf_op jit(solution)/shard_map/psum | solution.py:176
  315.0 78.4 %collective-permute-start.3 = (bf16[512,2048]{1,0:T(8,128)(2,1)}, bf16[512,2048]{1,0:T(8,128)(2,1)}, u32[]{:S(2)}, u32[]{:S(2)}) collective-permute-start(bf16[512,2048]{1,0:T(8,128)(2,1)} %bitcast.262), channel_id=1, source_target_pairs={{0,16},{16,0},{1,17},{17,1},{2,18},{18,2},{3,19},{19,3},{4,20},{20... | collective-permute-start | bytes 6291464 | tf_op jit(solution)/shard_map/ppermute | solution.py:18
  396.1 148.6 %all-gather.19.cloned.1.call-start = ((), (), s32[]{:S(2)}) async-start(), calls=%async_computation.11 | async-start | bytes 2621440 | tf_op jit(solution)/shard_map/all_gather | solution.py:166
  510.3 72.3 %all-gather.21.cloned.1.call-start = ((), (), s32[]{:S(2)}) async-start(), calls=%async_computation.12 | async-start | bytes 2621440 | tf_op jit(solution)/shard_map/all_gather | solution.py:167
  512.3 137.9 %reduce-scatter.11.cloned.1.call-start = ((), (), s32[]{:S(2)}) async-start(), calls=%async_computation.13 | async-start | bytes 5242880 | tf_op jit(solution)/shard_map/reduce_scatter | solution.py:209
  597.3 175.7 %all-reduce.8.cloned.1.call-start = ((), (), s32[]{:S(2)}) async-start(), calls=%async_computation.14 | async-start | bytes 4194304 | tf_op jit(solution)/shard_map/psum | solution.py:235
  686.3 169.1 %reduce-scatter.13.cloned.1.call-start = ((), (), s32[]{:S(2)}) async-start(), calls=%async_computation.15 | async-start | bytes 5242880 | tf_op jit(solution)/shard_map/reduce_scatter | solution.py:209
  802.3 245.9 %all-reduce.10.cloned.1.call-start = ((), (), s32[]{:S(2)}) async-start(), calls=%async_computation.26 | async-start | bytes 8388608 | tf_op jit(solution)/shard_map/psum | solution.py:235
  815.4 258.1 %collective-permute-start.18 = (bf16[2048,2048]{1,0:T(8,128)(2,1)}, bf16[2048,2048]{1,0:T(8,128)(2,1)}, u32[]{:S(2)}, u32[]{:S(2)}) collective-permute-start(bf16[2048,2048]{1,0:T(8,128)(2,1)} %get-tuple-element.169), channel_id=1, source_target_pairs={{0,16},{1,17},{2,18},{3,19},{4,20},{5,21},{6,22},{7,23},{8,24},{9,... | collective-permute-start | bytes 25165832 | tf_op jit(solution)/shard_map/ppermute | solution.py:14
  890.9 343.6 %reduce-scatter.19.cloned.1.call-start = ((), (), s32[]{:S(2)}) async-start(), calls=%async_computation.18 | async-start | bytes 2621440 | tf_op jit(solution)/shard_map/reduce_scatter | solution.py:313
  906.7 166.8 %collective-permute-start.17 = (bf16[2048,2048]{1,0:T(8,128)(2,1)}, bf16[2048,2048]{1,0:T(8,128)(2,1)}, u32[]{:S(2)}, u32[]{:S(2)}) collective-permute-start(bf16[2048,2048]{1,0:T(8,128)(2,1)} %get-tuple-element.171), channel_id=1, source_target_pairs={{16,0},{17,1},{18,2},{19,3},{20,4},{21,5},{22,6},{23,7},{24,8},{25... | collective-permute-start | bytes 25165832 | tf_op jit(solution)/shard_map/ppermute | solution.py:14
  928.2 308.4 %reduce-scatter.25.cloned.1.call-start = ((), (), s32[]{:S(2)}) async-start(), calls=%async_computation.25 | async-start | bytes 245760
  928.3 124.5 %collective-permute-start.14 = (bf16[2,768]{1,0:T(2,128)(2,1)S(1)}, bf16[2,768]{1,0:T(2,128)(2,1)S(1)}, u32[]{:S(2)}, u32[]{:S(2)}) collective-permute-start(bf16[2,768]{1,0:T(2,128)(2,1)S(1)} %convert_element_type.382), channel_id=1, source_target_pairs={{0,16},{1,17},{2,18},{3,19},{4,20},{5,21},{6,22},{7,23},{8,24},{9,... | collective-permute-start | bytes 9224 | tf_op jit(solution)/shard_map/ppermute | solution.py:14
  930.4 124.6 %collective-permute-start.10 = (bf16[5,2048]{1,0:T(8,128)(2,1)S(1)}, bf16[5,2048]{1,0:T(8,128)(2,1)S(1)}, u32[]{:S(2)}, u32[]{:S(2)}) collective-permute-start(bf16[5,2048]{1,0:T(8,128)(2,1)S(1)} %convert_element_type.372), channel_id=1, source_target_pairs={{0,16},{1,17},{2,18},{3,19},{4,20},{5,21},{6,22},{7,23},{8,24},{9,... | collective-permute-start | bytes 61448 | tf_op jit(solution)/shard_map/ppermute | solution.py:14
  931.8 122.3 %collective-permute-start.13 = (bf16[2,768]{1,0:T(2,128)(2,1)S(1)}, bf16[2,768]{1,0:T(2,128)(2,1)S(1)}, u32[]{:S(2)}, u32[]{:S(2)}) collective-permute-start(bf16[2,768]{1,0:T(2,128)(2,1)S(1)} %convert_element_type.380), channel_id=1, source_target_pairs={{16,0},{17,1},{18,2},{19,3},{20,4},{21,5},{22,6},{23,7},{24,8},{25... | collective-permute-start | bytes 9224 | tf_op jit(solution)/shard_map/ppermute | solution.py:14
  1055.0 183.1 %reduce-scatter.15.cloned.1.call-start = ((), (), s32[]{:S(2)}) async-start(), calls=%async_computation.16 | async-start | bytes 40960 | tf_op jit(solution)/shard_map/reduce_scatter | solution.py:313
  1073.4 176.8 %reduce-scatter.21.cloned.1.call-start = ((), (), s32[]{:S(2)}) async-start(), calls=%async_computation.19 | async-start | bytes 10485760 | tf_op jit(solution)/shard_map/reduce_scatter | solution.py:313
  1094.5 222.9 %reduce-scatter.23.cloned.1.call-start = ((), (), s32[]{:S(2)}) async-start(), calls=%async_computation.20 | async-start | bytes 10485760 | tf_op jit(solution)/shard_map/reduce_scatter | solution.py:313
  1103.9 18.2 %collective-permute-start.22 = (bf16[2048,2048]{1,0:T(8,128)(2,1)}, bf16[2048,2048]{1,0:T(8,128)(2,1)}, u32[]{:S(2)}, u32[]{:S(2)}) collective-permute-start(bf16[2048,2048]{1,0:T(8,128)(2,1)} %get-tuple-element.177), channel_id=1, source_target_pairs={{0,16},{1,17},{2,18},{3,19},{4,20},{5,21},{6,22},{7,23},{8,24},{9,... | collective-permute-start | bytes 25165832 | tf_op jit(solution)/shard_map/ppermute | solution.py:14
  1120.8 15.4 %collective-permute-start.21 = (bf16[2048,2048]{1,0:T(8,128)(2,1)}, bf16[2048,2048]{1,0:T(8,128)(2,1)}, u32[]{:S(2)}, u32[]{:S(2)}) collective-permute-start(bf16[2048,2048]{1,0:T(8,128)(2,1)} %get-tuple-element.179), channel_id=1, source_target_pairs={{16,0},{17,1},{18,2},{19,3},{20,4},{21,5},{22,6},{23,7},{24,8},{25... | collective-permute-start | bytes 25165832 | tf_op jit(solution)/shard_map/ppermute | solution.py:14
  1151.9 239.0 %reduce-scatter.17.cloned.1.call-start = ((), (), s32[]{:S(2)}) async-start(), calls=%async_computation.17 | async-start | bytes 7864320 | tf_op jit(solution)/shard_map/reduce_scatter | solution.py:313
  1207.4 32.2 %collective-permute-start.7 = (f32[2,256,2048]{2,1,0:T(8,128)}, f32[2,256,2048]{2,1,0:T(8,128)}, u32[]{:S(2)}, u32[]{:S(2)}) collective-permute-start(f32[2,256,2048]{2,1,0:T(8,128)} %bitcast.43), channel_id=1, source_target_pairs={{16,0},{17,1},{18,2},{19,3},{20,4},{21,5},{22,6},{23,7},{24,8},{25... | collective-permute-start | bytes 12582920 | tf_op jit(solution)/shard_map/ppermute | solution.py:14
  1211.5 28.1 %collective-permute-start.8 = (f32[2,256,2048]{2,1,0:T(8,128)}, f32[2,256,2048]{2,1,0:T(8,128)}, u32[]{:S(2)}, u32[]{:S(2)}) collective-permute-start(f32[2,256,2048]{2,1,0:T(8,128)} %bitcast.46), channel_id=1, source_target_pairs={{0,16},{1,17},{2,18},{3,19},{4,20},{5,21},{6,22},{7,23},{8,24},{9,... | collective-permute-start | bytes 12582920 | tf_op jit(solution)/shard_map/ppermute | solution.py:14
  (96 other events, 3081.6 us)
Sparse Core Ops, SparseCore 0:
  10.5 72.8 all-gather.22
  85.2 87.7 all-gather.28
  174.8 87.6 all-gather.26
  264.1 35.1 all-gather.24
  301.6 35.3 all-gather.16
  339.2 35.2 all-gather.14
  396.3 93.7 all-reduce.5
  510.5 34.2 all-gather.18
  547.3 35.2 all-gather.20
  597.4 52.6 reduce-scatter.10
  686.5 86.4 all-reduce.7
  802.4 52.9 reduce-scatter.12
  891.0 157.1 all-reduce.9
  1051.3 34.1 reduce-scatter.18
  1088.2 23.9 reduce-scatter.24
  1114.8 23.5 reduce-scatter.14
  1141.6 86.4 reduce-scatter.20
  1231.0 86.4 reduce-scatter.22
  1320.7 70.1 reduce-scatter.16

commit v2 on v1

--- a/solution.py
+++ b/solution.py
@@ -16,6 +16,33 @@
 
 def swap_sections(value):
     return lax.ppermute(value, "section", [(0, 1), (1, 0)])
+
+
+def causal_gather(block, axis):
+    count = lax.axis_size("ctx")
+    index = lax.axis_index("ctx")
+    width = block.shape[axis]
+    shape = list(block.shape)
+    shape[axis] = count * width
+    full = jnp.zeros(shape, block.dtype)
+    for shift in range(count - 1, 0, -1):
+        moved = lax.ppermute(block, "ctx", [(i, i + shift) for i in range(count - shift)])
+        full = lax.dynamic_update_slice_in_dim(full, moved, (index - shift) * width, axis)
+    return lax.dynamic_update_slice_in_dim(full, block, index * width, axis)
+
+
+def causal_return(full, axis):
+    count = lax.axis_size("ctx")
+    index = lax.axis_index("ctx")
+    width = full.shape[axis] // count
+    total = lax.dynamic_slice_in_dim(full, index * width, width, axis)
+    for shift in range(1, count):
+        piece = lax.dynamic_slice_in_dim(full, (index - shift) * width, width, axis)
+        moved = lax.ppermute(
+            piece.astype(jnp.bfloat16), "ctx", [(i + shift, i) for i in range(count - shift)]
+        )
+        total = total + moved.astype(jnp.float32)
+    return total
 
 
 def gelu_parts(values):
@@ -163,8 +190,7 @@
         jnp.bfloat16
     )
     value_rows = mixed_rows[..., 2 * head_dim :].astype(jnp.bfloat16)
-    key_all = lax.all_gather(key_rows, "ctx", axis=1, tiled=True)
-    value_all = lax.all_gather(value_rows, "ctx", axis=1, tiled=True)
+    key_all, value_all = causal_gather(jnp.stack([key_rows, value_rows]), 2)
     context, log_total = attend_heads(query_rows, key_all, value_all, allowed, score_scale)
     pre_act = jnp.dot(input_two, up_full, preferred_element_type=jnp.float32) + up_shift
     activated, slope = gelu_parts(pre_act)
@@ -180,7 +206,7 @@
     return result, saved
 
 
-def layer_backward(grad_rows, saved, weights, cosine, sine, allowed, score_scale):
+def layer_backward(grad_rows, saved, weights, cosine, sine, allowed, score_scale, tie):
     gains, _, qkv_full, qkv_shift, dense_full, up_full, down_full = weights
     (unit, inverse, input_one, input_two, query_rows, key_all, value_all, context, log_total,
      slope, active) = saved
@@ -206,12 +232,7 @@
     grad_query, grad_key_all, grad_value_all = attend_back(
         query_rows, key_all, value_all, context, log_total, grad_context, allowed, score_scale
     )
-    key_value_grads = lax.psum_scatter(
-        jnp.stack([grad_key_all, grad_value_all]).astype(jnp.bfloat16),
-        "ctx",
-        scatter_dimension=2,
-        tiled=True,
-    ).astype(jnp.float32)
+    key_value_grads = causal_return(jnp.stack([grad_key_all, grad_value_all]), 2)
     grad_mixed = jnp.concatenate(
         [
             rotate_back(grad_query, cosine, sine),
@@ -232,9 +253,9 @@
             jnp.sum(back_two, 0),
         ]
     )
-    scaled = lax.psum(
-        (back_one * gain_one + back_two * gain_two).astype(jnp.bfloat16), "tp"
-    ).astype(jnp.float32)
+    scaled = (back_one * gain_one + back_two * gain_two).astype(jnp.bfloat16)
+    tie, scaled = lax.optimization_barrier((tie, scaled))
+    scaled = lax.psum(scaled, "tp").astype(jnp.float32)
     first_mean = jnp.mean(scaled, axis=-1, keepdims=True)
     second_mean = jnp.mean(scaled * unit, axis=-1, keepdims=True)
     grad_input = grad_flat + inverse * (scaled - first_mean - unit * second_mean)
@@ -242,7 +263,51 @@
         [norm_terms, grad_out_shift[None]], 0
     )
     grad_terms = (small, grad_qkv, grad_qkv_shift, grad_dense, grad_up, grad_up_shift, grad_down)
-    return grad_input.reshape(seq_count, tok_rows, model_width), grad_terms
+    return grad_input.reshape(seq_count, tok_rows, model_width), grad_terms, tie
+
+
+SPLIT_AXES = (None, 2, None, 0, 1, None, 0)
+CTX_AXES = (1, 0, 1, 1, 0, 0, 1)
+
+
+def reduce_layer(terms, owner):
+    section_index = lax.axis_index("section")
+    ctx_count = lax.axis_size("ctx")
+    context_index = lax.axis_index("ctx")
+    small = terms[0]
+    small = jnp.concatenate([lax.psum(small[:4], "tp"), small[4:]], 0)
+    tiny = [small, terms[2], terms[5]]
+    tiny_axes = [1, 1, 0]
+    flat = []
+    sizes = []
+    for value, axis in zip(tiny, tiny_axes):
+        moved = jnp.moveaxis(value, axis, 0)
+        sizes.append(moved.shape)
+        flat.append(moved.reshape(ctx_count, -1))
+    packed = lax.psum(jnp.concatenate(flat, 1), ("section", "ctx"))
+    packed = lax.dynamic_index_in_dim(packed, context_index, 0, keepdims=False)
+    pieces = []
+    offset = 0
+    for shape, axis in zip(sizes, tiny_axes):
+        width = math.prod(shape) // ctx_count
+        piece = packed[offset : offset + width].reshape((shape[0] // ctx_count,) + shape[1:])
+        pieces.append(jnp.moveaxis(piece, 0, axis))
+        offset += width
+    out = [pieces[0], None, pieces[1], None, None, pieces[2], None]
+    for position in (1, 3, 4, 6):
+        value = terms[position]
+        split_axis = SPLIT_AXES[position]
+        half = value.shape[split_axis] // 2
+        mine = lax.dynamic_slice_in_dim(value, section_index * half, half, split_axis)
+        theirs = lax.dynamic_slice_in_dim(value, (1 - section_index) * half, half, split_axis)
+        summed = mine + swap_sections(theirs.astype(jnp.bfloat16)).astype(jnp.float32)
+        reduced = lax.psum_scatter(
+            summed.astype(jnp.bfloat16), "ctx", scatter_dimension=CTX_AXES[position], tiled=True
+        ).astype(jnp.float32)
+        moved = one_way(reduced, 1 - owner, owner)
+        halves = [reduced, moved] if owner == 0 else [moved, reduced]
+        out[position] = jnp.concatenate(halves, split_axis)
+    return tuple(out)
 
 
 def on_device(
@@ -285,42 +350,19 @@
     top, saved_second = layer_forward(
         mid.astype(jnp.bfloat16), second_layer, cosine, sine, allowed, score_scale
     )
+    grad_mid, terms_second, top = layer_backward(
+        grads, saved_second, second_layer, cosine, sine, allowed, score_scale, top
+    )
     top_other = one_way(top, 0, 1)
-
-    grad_mid, terms_second = layer_backward(
-        grads, saved_second, second_layer, cosine, sine, allowed, score_scale
-    )
-    second_other = tuple(one_way(t.astype(jnp.bfloat16), 0, 1) for t in terms_second)
-    grad_in, terms_first = layer_backward(
-        grad_mid, saved_first, first_layer, cosine, sine, allowed, score_scale
-    )
-    first_other = tuple(one_way(t.astype(jnp.bfloat16), 1, 0) for t in terms_first)
+    reduced_second = reduce_layer(terms_second, 1)
+    grad_in, terms_first, _ = layer_backward(
+        grad_mid, saved_first, first_layer, cosine, sine, allowed, score_scale, grad_mid
+    )
+    reduced_first = reduce_layer(terms_first, 0)
     grad_other = one_way(grad_in, 1, 0)
-
-    totals = tuple(
-        jnp.where(
-            section_index == 0,
-            a + b.astype(jnp.float32),
-            c + d.astype(jnp.float32),
-        )
-        for a, b, c, d in zip(terms_first, first_other, terms_second, second_other)
-    )
-    small, g_qkv, g_qkv_shift, g_dense, g_up, g_up_shift, g_down = totals
-    small = lax.psum(small[:4], "tp")
-    small = jnp.concatenate([small, totals[0][4:]], 0)
-
-    def scatter(value, axis):
-        return lax.psum_scatter(
-            value.astype(jnp.bfloat16), "ctx", scatter_dimension=axis, tiled=True
-        ).astype(jnp.float32)
-
-    small = scatter(small, 1)
-    g_qkv = scatter(g_qkv, 0)
-    g_qkv_shift = scatter(g_qkv_shift, 1)
-    g_dense = scatter(g_dense, 1)
-    g_up = scatter(g_up, 0)
-    g_up_shift = scatter(g_up_shift, 0)
-    g_down = scatter(g_down, 1)
+    small, g_qkv, g_qkv_shift, g_dense, g_up, g_up_shift, g_down = (
+        jnp.where(section_index == 0, a, b) for a, b in zip(reduced_first, reduced_second)
+    )
 
     block_ends = jnp.where(
         section_index == 0,

time: 1410 us -> 1500 us (1.064)
  waiting for transfers between devices: 817 us -> 883 us
  local copies, waits for them, and re-layouts: 98.2 us -> 137 us
  matrix products: 216 us -> 179 us
  other arithmetic: 155 us -> 186 us
  blocking collectives: 52.8 us -> 25 us
    ppermute x0 -> x12, waiting for transfers between devices: none -> 119 us  [the longest x6 62 us: causal_return(): lax.ppermute(piece.astype(jnp.bfloat16), 'ctx', [(i + shift, i) for i in...]
    all_gather x4 -> x0, waiting for transfers between devices: 108 us -> none  [the longest x2 65.5 us: layer_forward(): value_all = lax.all_gather(value_rows, 'ctx', axis=1, tiled=True)]
    reduce_scatter x7 -> x8, waiting for transfers between devices: 161 us -> 212 us  [reduce_layer(): lax.psum_scatter(summed.astype(jnp.bfloat16), 'ctx', scatter_dimension=CT...]
    unnamed x184 -> x222, local copies, waits for them, and re-layouts: 27.8 us -> 70.4 us
    ppermute x7 -> x15, waiting for transfers between devices: 0.93 us -> 34.3 us  [swap_sections(): return lax.ppermute(value, 'section', [(0, 1), (1, 0)])]
    ppermute x16 -> x10, waiting for transfers between devices: 32.7 us -> 0.03 us  [one_way(): return lax.ppermute(value, 'section', [(src, dst)])]
    all_gather x1, waiting for transfers between devices: 89.5 us -> 59.5 us  [gather_layer(): lax.all_gather(w_up[0], 'ctx', axis=0, tiled=True)]
    ppermute x0 -> x12, starting transfers between devices: none -> 27 us  [the longest x6 18 us: causal_gather(): lax.ppermute(block, 'ctx', [(i, i + shift) for i in range(count - shift)])]
  transfers between devices with their start and end apart: 42 -> 55, of which waited for: 20 -> 25; matrix products, arithmetic and copies ran while one was open for 25% -> 24% of each run, Pallas kernels for 0% -> 0%
where the time goes in v2:
time: 1500 us; the launch traced here: 1490 us
  waiting for transfers between devices  883 us (59%)
  other arithmetic  186 us (12%)
  matrix products  179 us (12%)
  local copies, waits for them, and re-layouts  137 us (9%)
  starting transfers between devices  61.7 us (4%)
  blocking collectives  25 us (2%)
  between operations  16.5 us (1%)
    reduce_scatter x8, waiting for transfers between devices, reduce_layer(): lax.psum_scatter(summed.astype(jnp.bfloat16), 'ctx', scatter_dimension=CT...  212 us
    psum x2, waiting for transfers between devices, layer_backward(): scaled = lax.psum(scaled, 'tp').astype(jnp.float32)  142 us
    psum x2, waiting for transfers between devices, layer_forward(): lax.psum(partial_sum.astype(jnp.bfloat16), 'tp').astype(jnp.float32)  99 us
    all_gather x1, waiting for transfers between devices, gather_layer(): lax.all_gather(w_down[0], 'ctx', axis=1, tiled=True)  86.5 us
    all_gather x1, waiting for transfers between devices, gather_layer(): lax.all_gather(w_qkv[0], 'ctx', axis=0, tiled=True)  73.3 us
    unnamed x222, local copies, waits for them, and re-layouts  70.4 us
    dot_general x8, matrix products, dot_transposed(): lax.dot_general(left, right, (((1,), (1,)), ((), ())), preferred_element_...  64.1 us
    ppermute x6, waiting for transfers between devices, causal_return(): lax.ppermute(piece.astype(jnp.bfloat16), 'ctx', [(i + shift, i) for i in...  62 us
  transfers between devices with their start and end apart: 55, of which 25 were waited for; matrix products, arithmetic and copies ran while one was open for 24% of the time, Pallas kernels for 0%

profile of v2, /device:TPU:0, one launch (start us, length us, event | category | flops | bytes accessed | tf_op | source)
XLA Modules:
  0.0 1488.1 jit_solution(15769712641426534717)
XLA Ops:
  9.5 73.3 %all-gather.11.cloned.1.call-done = bf16[1,2048,2,768]{3,2,0,1:T(2,128)(2,1)} async-done(((bf16[1,512,2,768]{3,2,0,1:T(2,128)(2,1)}), bf16[1,2048,2,768]{3,2,0,1:T(2,128)(2,1)}) %all-gather.11.cloned.1.call-update) | async-done | bytes 6291472 | tf_op jit(solution)/shard_map/all_gather | solution.py:158
  83.0 9.6 all-gather.1
  100.4 8.0 all-gather.4
  113.1 59.5 %all-gather.15.cloned.1.call-done = bf16[1,2048,2048]{2,1,0:T(8,128)(2,1)} async-done(((bf16[1,512,2048]{2,1,0:T(8,128)(2,1)}), bf16[1,2048,2048]{2,1,0:T(8,128)(2,1)}) %all-gather.15.cloned.1.call-update) | async-done | bytes 8388624 | tf_op jit(solution)/shard_map/all_gather | solution.py:161
  175.4 86.5 %all-gather.17.cloned.1.call-done = bf16[1,2048,2048]{2,1,0:T(8,128)(2,1)} async-done(((bf16[1,2048,512]{2,1,0:T(8,128)(2,1)}), bf16[1,2048,2048]{2,1,0:T(8,128)(2,1)}) %all-gather.17.cloned.1.call-update) | async-done | bytes 8388624 | tf_op jit(solution)/shard_map/all_gather | solution.py:162
  262.0 12.9 broadcast_select_fusion.1
  309.7 14.4 collective-permute-done.3
  325.8 22.6 %collective-permute-done.4 = bf16[2,2,256,2,256]{4,2,3,1,0:T(8,128)(2,1)} collective-permute-done((bf16[2,2,256,2,256]{4,2,3,1,0:T(8,128)(2,1)}, bf16[2,2,256,2,256]{4,2,3,1,0:T(8,128)(2,1)}, u32[]{:S(2)}, u32[]{:S(2)}) %collective-permute-start.4) | collective-permute-done | bytes 1048608 | tf_op jit(solution)/shard_map/ppermute | solution.py:29
  356.8 10.8 fusion.53
  396.5 74.3 %all-reduce.9.cloned.1.call-done = bf16[512,2048]{1,0:T(8,128)(2,1)} async-done(((bf16[512,2048]{1,0:T(8,128)(2,1)}), bf16[512,2048]{1,0:T(8,128)(2,1)}) %all-reduce.9.cloned.1.call-update) | async-done | bytes 2097168 | tf_op jit(solution)/shard_map/psum | solution.py:202
  494.4 8.5 fusion.56
  502.9 12.7 fusion.165
  516.0 20.5 %collective-permute-done.11 = bf16[2,2,256,2,256]{4,2,3,1,0:T(8,128)(2,1)S(1)} collective-permute-done((bf16[2,2,256,2,256]{4,2,3,1,0:T(8,128)(2,1)S(1)}, bf16[2,2,256,2,256]{4,2,3,1,0:T(8,128)(2,1)S(1)}, u32[]{:S(2)}, u32[]{:S(2)}) %collective-permute-start.11) | collective-permute-done | bytes 1048608 | tf_op jit(solution)/shard_map/ppermute | solution.py:29
  554.3 10.2 fusion.57
  579.2 20.5 %collective-permute-done.14 = bf16[2,2,256,2,256]{4,2,3,1,0:T(8,128)(2,1)} collective-permute-done((bf16[2,2,256,2,256]{4,2,3,1,0:T(8,128)(2,1)}, bf16[2,2,256,2,256]{4,2,3,1,0:T(8,128)(2,1)}, u32[]{:S(2)}, u32[]{:S(2)}) %collective-permute-start.14) | collective-permute-done | bytes 1048608 | tf_op jit(solution)/shard_map/ppermute | solution.py:41
  625.9 13.0 add_convert_fusion.7
  638.9 24.7 %all-reduce.11.cloned.1.call-done = bf16[512,2048]{1,0:T(8,128)(2,1)} async-done(((bf16[512,2048]{1,0:T(8,128)(2,1)}), bf16[512,2048]{1,0:T(8,128)(2,1)}) %all-reduce.11.cloned.1.call-update) | async-done | bytes 2097168 | tf_op jit(solution)/shard_map/psum | solution.py:202
  668.2 85.4 %all-reduce.13.cloned.1.call-done = bf16[512,2048]{1,0:T(8,128)(2,1)} async-done(((bf16[512,2048]{1,0:T(8,128)(2,1)}), bf16[512,2048]{1,0:T(8,128)(2,1)}) %all-reduce.13.cloned.1.call-update) | async-done | bytes 2097168 | tf_op jit(solution)/shard_map/psum | solution.py:258
  788.6 10.7 fusion.166
  799.3 13.2 collective-permute-done.18
  812.5 22.7 %collective-permute-done.17 = bf16[2,2,256,2,256]{4,2,3,1,0:T(8,128)(2,1)S(1)} collective-permute-done((bf16[2,2,256,2,256]{4,2,3,1,0:T(8,128)(2,1)S(1)}, bf16[2,2,256,2,256]{4,2,3,1,0:T(8,128)(2,1)S(1)}, u32[]{:S(2)}, u32[]{:S(2)}) %collective-permute-start.17) | collective-permute-done | bytes 1048608 | tf_op jit(solution)/shard_map/ppermute | solution.py:41
  857.1 11.8 add_convert_fusion.6
  899.8 56.2 %all-reduce.15.cloned.1.call-done = bf16[512,2048]{1,0:T(8,128)(2,1)} async-done(((bf16[512,2048]{1,0:T(8,128)(2,1)}), bf16[512,2048]{1,0:T(8,128)(2,1)}) %all-reduce.15.cloned.1.call-update) | async-done | bytes 2097168 | tf_op jit(solution)/shard_map/psum | solution.py:258
  984.7 7.5 collective-permute-done.31
  992.2 8.5 add_convert_fusion.2
  1142.1 14.1 reduce-scatter.19.cloned.1.call-done
  1160.0 51.7 %reduce-scatter.23.cloned.1.call-done = bf16[1024,512]{1,0:T(8,128)(2,1)} async-done(((bf16[1024,2048]{1,0:T(8,128)(2,1)}), bf16[1024,512]{1,0:T(8,128)(2,1)}) %reduce-scatter.23.cloned.1.call-update) | async-done | bytes 1048592 | tf_op jit(solution)/shard_map/reduce_scatter | solution.py:304
  1214.8 44.6 %reduce-scatter.9.cloned.1.call-done = bf16[512,2,384]{2,0,1:T(8,128)(2,1)} async-done(((bf16[2048,2,384]{2,0,1:T(8,128)(2,1)}), bf16[512,2,384]{2,0,1:T(8,128)(2,1)}) %reduce-scatter.9.cloned.1.call-update) | async-done | bytes 786448 | tf_op jit(solution)/shard_map/reduce_scatter | solution.py:304
  1262.4 53.4 %reduce-scatter.17.cloned.1.call-done = bf16[512,1024]{1,0:T(8,128)(2,1)} async-done(((bf16[2048,1024]{1,0:T(8,128)(2,1)}), bf16[512,1024]{1,0:T(8,128)(2,1)}) %reduce-scatter.17.cloned.1.call-update) | async-done | bytes 1048592 | tf_op jit(solution)/shard_map/reduce_scatter | solution.py:304
  1323.9 47.9 %reduce-scatter.21.cloned.1.call-done = bf16[1024,512]{1,0:T(8,128)(2,1)} async-done(((bf16[1024,2048]{1,0:T(8,128)(2,1)}), bf16[1024,512]{1,0:T(8,128)(2,1)}) %reduce-scatter.21.cloned.1.call-update) | async-done | bytes 1048592 | tf_op jit(solution)/shard_map/reduce_scatter | solution.py:304
  1383.2 55.1 %all-reduce.17.cloned.1.call-done = (f32[4,3456]{1,0:T(4,128)}, f32[4,3456]{1,0:T(4,128)}) async-done(((f32[4,3456]{1,0:T(4,128)}, f32[4,3456]{1,0:T(4,128)}), (f32[4,3456]{1,0:T(4,128)}, f32[4,3456]{1,0:T(4,128)})) %all-reduce.17.cloned.1.call-update) | async-done | bytes 110608 | tf_op jit(solution)/shard_map/psum | solution.py:287
  1454.3 9.8 maximum_select_fusion
  (512 shorter events, 496.8 us)
Async XLA Ops:
  7.2 75.6 %all-gather.11.cloned.1.call-start = ((), (), s32[]{:S(2)}) async-start(), calls=%async_computation.20 | async-start | bytes 7864320 | tf_op jit(solution)/shard_map/all_gather | solution.py:158
  8.0 164.6 %all-gather.15.cloned.1.call-start = ((), (), s32[]{:S(2)}) async-start(), calls=%async_computation.22 | async-start | bytes 10485760 | tf_op jit(solution)/shard_map/all_gather | solution.py:161
  8.7 253.2 %all-gather.17.cloned.1.call-start = ((), (), s32[]{:S(2)}) async-start(), calls=%async_computation.23 | async-start | bytes 10485760 | tf_op jit(solution)/shard_map/all_gather | solution.py:162
  9.5 300.2 %all-gather.13.cloned.1.call-start = ((), (), s32[]{:S(2)}) async-start(), calls=%async_computation.21 | async-start | bytes 2621440 | tf_op jit(solution)/shard_map/all_gather | solution.py:160
  82.8 179.1 %collective-permute-start.1 = (bf16[2048,2,768]{2,1,0:T(2,128)(2,1)}, bf16[2048,2,768]{2,1,0:T(2,128)(2,1)}, u32[]{:S(2)}, u32[]{:S(2)}) collective-permute-start(bf16[2048,2,768]{2,1,0:T(2,128)(2,1)} %bitcast.340), channel_id=1, source_target_pairs={{0,16},{16,0},{1,17},{17,1},{2,18},{18,2},{3,19},{19,3},{4,20},{20... | collective-permute-start | bytes 18874376 | tf_op jit(solution)/shard_map/ppermute | solution.py:18
  108.5 195.9 %collective-permute-start.8 = (bf16[2048]{0:T(1024)(128)(2,1)S(1)}, bf16[2048]{0:T(1024)(128)(2,1)S(1)}, u32[]{:S(2)}, u32[]{:S(2)}) collective-permute-start(bf16[2048]{0:T(1024)(128)(2,1)S(1)} %reduce.3), channel_id=1, source_target_pairs={{0,16},{16,0},{1,17},{17,1},{2,18},{18,2},{3,19},{19,3},{4,20},{20... | collective-permute-start | bytes 12296 | tf_op jit(solution)/shard_map/ppermute | solution.py:18
  108.6 362.2 %all-reduce.9.cloned.1.call-start = ((), (), s32[]{:S(2)}) async-start(), calls=%async_computation.8 | async-start | bytes 4194304 | tf_op jit(solution)/shard_map/psum | solution.py:202
  172.6 184.2 %collective-permute-start.7 = (bf16[2048,2048]{1,0:T(8,128)(2,1)}, bf16[2048,2048]{1,0:T(8,128)(2,1)}, u32[]{:S(2)}, u32[]{:S(2)}) collective-permute-start(bf16[2048,2048]{1,0:T(8,128)(2,1)} %bitcast.387), channel_id=1, source_target_pairs={{0,16},{16,0},{1,17},{17,1},{2,18},{18,2},{3,19},{19,3},{4,20},{20... | collective-permute-start | bytes 25165832 | tf_op jit(solution)/shard_map/ppermute | solution.py:18
  262.0 105.7 %collective-permute-start.9 = (bf16[2048,2048]{1,0:T(8,128)(2,1)}, bf16[2048,2048]{1,0:T(8,128)(2,1)}, u32[]{:S(2)}, u32[]{:S(2)}) collective-permute-start(bf16[2048,2048]{1,0:T(8,128)(2,1)} %bitcast.388), channel_id=1, source_target_pairs={{0,16},{16,0},{1,17},{17,1},{2,18},{18,2},{3,19},{19,3},{4,20},{20... | collective-permute-start | bytes 25165832 | tf_op jit(solution)/shard_map/ppermute | solution.py:18
  377.3 286.3 %all-reduce.11.cloned.1.call-start = ((), (), s32[]{:S(2)}) async-start(), calls=%async_computation.9 | async-start | bytes 4194304 | tf_op jit(solution)/shard_map/psum | solution.py:202
  573.4 180.1 %all-reduce.13.cloned.1.call-start = ((), (), s32[]{:S(2)}) async-start(), calls=%async_computation.10 | async-start | bytes 4194304 | tf_op jit(solution)/shard_map/psum | solution.py:258
  667.9 288.1 %all-reduce.15.cloned.1.call-start = ((), (), s32[]{:S(2)}) async-start(), calls=%async_computation.11 | async-start | bytes 4194304 | tf_op jit(solution)/shard_map/psum | solution.py:258
  868.9 251.4 %reduce-scatter.15.cloned.1.call-start = ((), (), s32[]{:S(2)}) async-start(), calls=%async_computation.15 | async-start | bytes 1310720 | tf_op jit(solution)/shard_map/reduce_scatter | solution.py:304
  883.6 244.9 %reduce-scatter.13.cloned.1.call-start = ((), (), s32[]{:S(2)}) async-start(), calls=%async_computation.14 | async-start | bytes 1310720 | tf_op jit(solution)/shard_map/reduce_scatter | solution.py:304
  899.1 232.6 %all-reduce.19.cloned.1.call-start = ((), (), s32[]{:S(2)}) async-start(), calls=%async_computation.25 | async-start | bytes 131072 | tf_op jit(solution)/shard_map/psum | solution.py:278
  962.2 171.2 %reduce-scatter.11.cloned.1.call-start = ((), (), s32[]{:S(2)}) async-start(), calls=%async_computation.13 | async-start | bytes 3932160 | tf_op jit(solution)/shard_map/reduce_scatter | solution.py:304
  968.7 187.5 %reduce-scatter.19.cloned.1.call-start = ((), (), s32[]{:S(2)}) async-start(), calls=%async_computation.17 | async-start | bytes 5242880 | tf_op jit(solution)/shard_map/reduce_scatter | solution.py:304
  1000.7 211.0 %reduce-scatter.23.cloned.1.call-start = ((), (), s32[]{:S(2)}) async-start(), calls=%async_computation.19 | async-start | bytes 5242880 | tf_op jit(solution)/shard_map/reduce_scatter | solution.py:304
  1031.4 228.0 %reduce-scatter.9.cloned.1.call-start = ((), (), s32[]{:S(2)}) async-start(), calls=%async_computation.12 | async-start | bytes 3932160 | tf_op jit(solution)/shard_map/reduce_scatter | solution.py:304
  1048.5 267.3 %reduce-scatter.17.cloned.1.call-start = ((), (), s32[]{:S(2)}) async-start(), calls=%async_computation.16 | async-start | bytes 5242880 | tf_op jit(solution)/shard_map/reduce_scatter | solution.py:304
  1078.5 293.3 %reduce-scatter.21.cloned.1.call-start = ((), (), s32[]{:S(2)}) async-start(), calls=%async_computation.18 | async-start | bytes 5242880 | tf_op jit(solution)/shard_map/reduce_scatter | solution.py:304
  1109.2 329.1 %all-reduce.17.cloned.1.call-start = ((), (), s32[]{:S(2)}) async-start(), calls=%async_computation.24 | async-start | bytes 221184 | tf_op jit(solution)/shard_map/psum | solution.py:287
  1109.2 213.4 %collective-permute-start.20 = (f32[2,256,2048]{2,1,0:T(8,128)}, f32[2,256,2048]{2,1,0:T(8,128)}, u32[]{:S(2)}, u32[]{:S(2)}) collective-permute-start(f32[2,256,2048]{2,1,0:T(8,128)} %bitcast.320), channel_id=1, source_target_pairs={{0,16},{1,17},{2,18},{3,19},{4,20},{5,21},{6,22},{7,23},{8,24},{9,... | collective-permute-start | bytes 12582920 | tf_op jit(solution)/shard_map/ppermute | solution.py:14
  1118.5 260.2 %collective-permute-start.19 = (f32[2,256,2048]{2,1,0:T(8,128)}, f32[2,256,2048]{2,1,0:T(8,128)}, u32[]{:S(2)}, u32[]{:S(2)}) collective-permute-start(f32[2,256,2048]{2,1,0:T(8,128)} %bitcast.54), channel_id=1, source_target_pairs={{16,0},{17,1},{18,2},{19,3},{20,4},{21,5},{22,6},{23,7},{24,8},{25... | collective-permute-start | bytes 12582920 | tf_op jit(solution)/shard_map/ppermute | solution.py:14
  1122.2 197.3 %collective-permute-start.28 = (f32[256,512]{1,0:T(8,128)S(1)}, f32[256,512]{1,0:T(8,128)}, u32[]{:S(2)}, u32[]{:S(2)}) collective-permute-start(f32[256,512]{1,0:T(8,128)S(1)} %get-tuple-element.151), channel_id=1, source_target_pairs={{0,16},{1,17},{2,18},{3,19},{4,20},{5,21},{6,22},{7,23},{8,24},{9,... | collective-permute-start | bytes 1572872 | tf_op jit(solution)/shard_map/ppermute | solution.py:14
  1130.4 245.3 %collective-permute-start.26 = (f32[256,512]{1,0:T(8,128)S(1)}, f32[256,512]{1,0:T(8,128)}, u32[]{:S(2)}, u32[]{:S(2)}) collective-permute-start(f32[256,512]{1,0:T(8,128)S(1)} %get-tuple-element.154), channel_id=1, source_target_pairs={{16,0},{17,1},{18,2},{19,3},{20,4},{21,5},{22,6},{23,7},{24,8},{25... | collective-permute-start | bytes 1572872 | tf_op jit(solution)/shard_map/ppermute | solution.py:14
  1136.4 243.5 %collective-permute-start.24 = (f32[512,2,384]{2,0,1:T(8,128)}, f32[512,2,384]{2,0,1:T(8,128)}, u32[]{:S(2)}, u32[]{:S(2)}) collective-permute-start(f32[512,2,384]{2,0,1:T(8,128)} %get-tuple-element.134), channel_id=1, source_target_pairs={{0,16},{1,17},{2,18},{3,19},{4,20},{5,21},{6,22},{7,23},{8,24},{9,... | collective-permute-start | bytes 4718600 | tf_op jit(solution)/shard_map/ppermute | solution.py:14
  1319.5 151.0 %collective-permute-start.32 = (f32[512,1024]{1,0:T(8,128)}, f32[512,1024]{1,0:T(8,128)}, u32[]{:S(2)}, u32[]{:S(2)}) collective-permute-start(f32[512,1024]{1,0:T(8,128)} %get-tuple-element.130), channel_id=1, source_target_pairs={{0,16},{1,17},{2,18},{3,19},{4,20},{5,21},{6,22},{7,23},{8,24},{9,... | collective-permute-start | bytes 6291464 | tf_op jit(solution)/shard_map/ppermute | solution.py:14
  1322.6 147.9 %collective-permute-start.30 = (f32[512,1024]{1,0:T(8,128)}, f32[512,1024]{1,0:T(8,128)}, u32[]{:S(2)}, u32[]{:S(2)}) collective-permute-start(f32[512,1024]{1,0:T(8,128)} %get-tuple-element.133), channel_id=1, source_target_pairs={{16,0},{17,1},{18,2},{19,3},{20,4},{21,5},{22,6},{23,7},{24,8},{25... | collective-permute-start | bytes 6291464 | tf_op jit(solution)/shard_map/ppermute | solution.py:14
  1375.6 100.0 %collective-permute-start.36 = (f32[1024,512]{1,0:T(8,128)}, f32[1024,512]{1,0:T(8,128)}, u32[]{:S(2)}, u32[]{:S(2)}) collective-permute-start(f32[1024,512]{1,0:T(8,128)} %get-tuple-element.126), channel_id=1, source_target_pairs={{0,16},{1,17},{2,18},{3,19},{4,20},{5,21},{6,22},{7,23},{8,24},{9,... | collective-permute-start | bytes 6291464 | tf_op jit(solution)/shard_map/ppermute | solution.py:14
  1378.7 85.4 %collective-permute-start.22 = (f32[512,2,384]{2,0,1:T(8,128)}, f32[512,2,384]{2,0,1:T(8,128)}, u32[]{:S(2)}, u32[]{:S(2)}) collective-permute-start(f32[512,2,384]{2,0,1:T(8,128)} %get-tuple-element.137), channel_id=1, source_target_pairs={{16,0},{17,1},{18,2},{19,3},{20,4},{21,5},{22,6},{23,7},{24,8},{25... | collective-permute-start | bytes 4718600 | tf_op jit(solution)/shard_map/ppermute | solution.py:14
  1380.0 95.7 %collective-permute-start.34 = (f32[1024,512]{1,0:T(8,128)}, f32[1024,512]{1,0:T(8,128)}, u32[]{:S(2)}, u32[]{:S(2)}) collective-permute-start(f32[1024,512]{1,0:T(8,128)} %get-tuple-element.129), channel_id=1, source_target_pairs={{16,0},{17,1},{18,2},{19,3},{20,4},{21,5},{22,6},{23,7},{24,8},{25... | collective-permute-start | bytes 6291464 | tf_op jit(solution)/shard_map/ppermute | solution.py:14
  (126 other events, 4021.0 us)
Sparse Core Ops, SparseCore 0:
  9.9 72.8 all-gather.10
  84.7 87.9 all-gather.14
  174.5 87.4 all-gather.16
  263.6 35.1 all-gather.12
  377.4 93.3 all-reduce.8
  573.6 90.0 all-reduce.10
  668.1 85.4 all-reduce.12
  869.1 86.8 all-reduce.14
  958.9 26.6 reduce-scatter.14
  989.2 27.7 reduce-scatter.12
  1019.3 34.0 all-reduce.18
  1056.5 43.6 reduce-scatter.10
  1103.5 52.6 reduce-scatter.18
  1159.0 52.6 reduce-scatter.22
  1215.4 43.9 reduce-scatter.8
  1263.0 52.6 reduce-scatter.16
  1319.2 52.6 reduce-scatter.20
  1383.3 54.9 all-reduce.16

commit v3 on v2

--- a/solution.py
+++ b/solution.py
@@ -146,128 +146,71 @@
     return (grad_query, grad_key, grad_value)
 
 
-def gather_layer(ln1_gain, ln1_bias, ln2_gain, ln2_bias, w_qkv, qkv_bias, w_dense, w_up,
-                 up_bias, w_down, out_bias):
-    gains = lax.all_gather(
-        jnp.concatenate([ln1_gain, ln1_bias, ln2_gain, ln2_bias, out_bias], 0),
-        "ctx", axis=1, tiled=True,
-    )
-    return (
-        gains,
-        lax.all_gather(up_bias[0], "ctx", axis=0, tiled=True),
-        lax.all_gather(w_qkv[0], "ctx", axis=0, tiled=True),
-        lax.all_gather(qkv_bias[0], "ctx", axis=1, tiled=True),
-        lax.all_gather(w_dense[0], "ctx", axis=1, tiled=True),
-        lax.all_gather(w_up[0], "ctx", axis=0, tiled=True),
-        lax.all_gather(w_down[0], "ctx", axis=1, tiled=True),
-    )
-
-
-def layer_forward(rows, weights, cosine, sine, allowed, score_scale):
-    gains, up_shift, qkv_full, qkv_shift, dense_full, up_full, down_full = weights
-    seq_count, tok_rows, model_width = rows.shape
-    head_count = qkv_full.shape[1]
-    head_dim = qkv_full.shape[2] // 3
-    flat_count = seq_count * tok_rows
-    gain_one, bias_one, gain_two, bias_two, out_shift = (
-        gains[i].astype(jnp.float32) for i in range(5)
-    )
-    up_shift = up_shift.astype(jnp.float32)
-    flat_rows = rows.reshape(flat_count, model_width).astype(jnp.float32)
-    row_mean = jnp.mean(flat_rows, axis=-1, keepdims=True)
-    centered = flat_rows - row_mean
-    row_var = jnp.mean(centered * centered, axis=-1, keepdims=True)
-    inverse = lax.rsqrt(row_var + norm_eps)
-    unit = centered * inverse
-    input_one = (unit * gain_one + bias_one).astype(jnp.bfloat16)
-    input_two = (unit * gain_two + bias_two).astype(jnp.bfloat16)
-    mixed_rows = jnp.dot(
-        input_one, qkv_full.reshape(model_width, -1), preferred_element_type=jnp.float32
-    ) + qkv_shift.astype(jnp.float32).reshape(-1)
-    mixed_rows = mixed_rows.reshape(seq_count, tok_rows, head_count, 3 * head_dim)
-    query_rows = rotate_heads(mixed_rows[..., :head_dim], cosine, sine).astype(jnp.bfloat16)
-    key_rows = rotate_heads(mixed_rows[..., head_dim : 2 * head_dim], cosine, sine).astype(
-        jnp.bfloat16
-    )
-    value_rows = mixed_rows[..., 2 * head_dim :].astype(jnp.bfloat16)
-    key_all, value_all = causal_gather(jnp.stack([key_rows, value_rows]), 2)
-    context, log_total = attend_heads(query_rows, key_all, value_all, allowed, score_scale)
-    pre_act = jnp.dot(input_two, up_full, preferred_element_type=jnp.float32) + up_shift
-    activated, slope = gelu_parts(pre_act)
-    active = activated.astype(jnp.bfloat16)
-    partial_sum = jnp.dot(
-        context.reshape(flat_count, -1), dense_full, preferred_element_type=jnp.float32
-    )
-    partial_sum = partial_sum + jnp.dot(active, down_full, preferred_element_type=jnp.float32)
-    branch = lax.psum(partial_sum.astype(jnp.bfloat16), "tp").astype(jnp.float32)
-    result = (flat_rows + branch + out_shift).reshape(seq_count, tok_rows, model_width)
-    saved = (unit, inverse, input_one, input_two, query_rows, key_all, value_all, context,
-             log_total, slope, active)
-    return result, saved
-
-
-def layer_backward(grad_rows, saved, weights, cosine, sine, allowed, score_scale, tie):
-    gains, _, qkv_full, qkv_shift, dense_full, up_full, down_full = weights
-    (unit, inverse, input_one, input_two, query_rows, key_all, value_all, context, log_total,
-     slope, active) = saved
-    seq_count, tok_rows, model_width = grad_rows.shape
-    head_count = qkv_full.shape[1]
-    head_dim = qkv_full.shape[2] // 3
-    flat_count = seq_count * tok_rows
-    gain_one = gains[0].astype(jnp.float32)
-    gain_two = gains[2].astype(jnp.float32)
-    grad_flat = grad_rows.reshape(flat_count, model_width)
-    grad_half = grad_flat.astype(jnp.bfloat16)
-    grad_out_shift = jnp.sum(grad_flat, 0)
-    grad_down = transposed_dot(active, grad_half)
-    grad_pre = dot_transposed(grad_half, down_full) * slope
-    grad_up_shift = jnp.sum(grad_pre, 0)
-    pre_half = grad_pre.astype(jnp.bfloat16)
-    grad_up = transposed_dot(input_two, pre_half)
-    back_two = dot_transposed(pre_half, up_full)
-    grad_dense = transposed_dot(context.reshape(flat_count, -1), grad_half)
-    grad_context = dot_transposed(grad_half, dense_full).reshape(
-        seq_count, tok_rows, head_count, head_dim
-    )
-    grad_query, grad_key_all, grad_value_all = attend_back(
-        query_rows, key_all, value_all, context, log_total, grad_context, allowed, score_scale
-    )
-    key_value_grads = causal_return(jnp.stack([grad_key_all, grad_value_all]), 2)
-    grad_mixed = jnp.concatenate(
-        [
-            rotate_back(grad_query, cosine, sine),
-            rotate_back(key_value_grads[0], cosine, sine),
-            key_value_grads[1],
-        ],
-        -1,
-    )
-    grad_qkv_shift = jnp.sum(grad_mixed, (0, 1))
-    mixed_half = grad_mixed.reshape(flat_count, -1).astype(jnp.bfloat16)
-    grad_qkv = transposed_dot(input_one, mixed_half).reshape(qkv_full.shape)
-    back_one = dot_transposed(mixed_half, qkv_full.reshape(model_width, -1))
-    norm_terms = jnp.stack(
-        [
-            jnp.sum(back_one * unit, 0),
-            jnp.sum(back_one, 0),
-            jnp.sum(back_two * unit, 0),
-            jnp.sum(back_two, 0),
-        ]
-    )
-    scaled = (back_one * gain_one + back_two * gain_two).astype(jnp.bfloat16)
-    tie, scaled = lax.optimization_barrier((tie, scaled))
-    scaled = lax.psum(scaled, "tp").astype(jnp.float32)
-    first_mean = jnp.mean(scaled, axis=-1, keepdims=True)
-    second_mean = jnp.mean(scaled * unit, axis=-1, keepdims=True)
-    grad_input = grad_flat + inverse * (scaled - first_mean - unit * second_mean)
-    small = jnp.concatenate(
-        [norm_terms, grad_out_shift[None]], 0
-    )
-    grad_terms = (small, grad_qkv, grad_qkv_shift, grad_dense, grad_up, grad_up_shift, grad_down)
-    return grad_input.reshape(seq_count, tok_rows, model_width), grad_terms, tie
-
-
-SPLIT_AXES = (None, 2, None, 0, 1, None, 0)
-CTX_AXES = (1, 0, 1, 1, 0, 0, 1)
+def section_pairs(owner, shift):
+    count = lax.axis_size("ctx")
+    return [(owner * count + i, owner * count + (i + shift) % count) for i in range(count)]
+
+
+def owner_gather(shard, owner, axis):
+    count = lax.axis_size("ctx")
+    index = lax.axis_index("ctx")
+    width = shard.shape[axis]
+    shape = list(shard.shape)
+    shape[axis] = count * width
+    full = lax.dynamic_update_slice_in_dim(jnp.zeros(shape, shard.dtype), shard, index * width, axis)
+    for shift in range(1, count):
+        moved = lax.ppermute(shard, ("section", "ctx"), section_pairs(owner, shift))
+        full = lax.dynamic_update_slice_in_dim(
+            full, moved, lax.rem(index - shift + count, count) * width, axis
+        )
+    return full
+
+
+def owner_scatter(total, owner, axis):
+    count = lax.axis_size("ctx")
+    index = lax.axis_index("ctx")
+    width = total.shape[axis] // count
+    result = lax.dynamic_slice_in_dim(total, index * width, width, axis)
+    for shift in range(1, count):
+        piece = lax.dynamic_slice_in_dim(
+            total, lax.rem(index + shift, count) * width, width, axis
+        )
+        moved = lax.ppermute(
+            piece.astype(jnp.bfloat16), ("section", "ctx"), section_pairs(owner, shift)
+        )
+        result = result + moved.astype(jnp.float32)
+    return result
+
+
+def layer_weights(params, owner):
+    (ln1_gain, ln1_bias, ln2_gain, ln2_bias, w_qkv, qkv_bias, w_dense, w_up, up_bias, w_down,
+     out_bias) = params
+    section_index = lax.axis_index("section")
+    count = lax.axis_size("ctx")
+    gains = jnp.concatenate([ln1_gain, ln1_bias, ln2_gain, ln2_bias, out_bias], 0)
+    packed = jnp.concatenate(
+        [gains.reshape(-1), up_bias.reshape(-1), qkv_bias.reshape(-1)]
+    )[None]
+    packed = owner_gather(packed, owner, 0)
+    gain_size = gains.size
+    bias_size = up_bias.size
+    gains_full = packed[:, :gain_size].reshape(count, 5, -1).transpose(1, 0, 2).reshape(5, -1)
+    up_full_shift = packed[:, gain_size : gain_size + bias_size].reshape(-1)
+    qkv_shift = packed[:, gain_size + bias_size :].reshape((count,) + qkv_bias.shape[1:])
+    qkv_shift = qkv_shift.transpose(1, 0, 2).reshape(qkv_bias.shape[1], -1)
+    pieces = (
+        gains_full,
+        up_full_shift,
+        owner_gather(w_qkv[0], owner, 0),
+        qkv_shift,
+        owner_gather(w_dense[0], owner, 1),
+        owner_gather(w_up[0], owner, 0),
+        owner_gather(w_down[0], owner, 1),
+    )
+    return tuple(
+        jnp.where(section_index == owner, piece, one_way(piece, owner, 1 - owner))
+        for piece in pieces
+    )
 
 
 def reduce_layer(terms, owner):
@@ -294,20 +237,114 @@
         pieces.append(jnp.moveaxis(piece, 0, axis))
         offset += width
     out = [pieces[0], None, pieces[1], None, None, pieces[2], None]
-    for position in (1, 3, 4, 6):
+    for position, axis in ((6, 1), (4, 0), (3, 1), (1, 0)):
         value = terms[position]
-        split_axis = SPLIT_AXES[position]
-        half = value.shape[split_axis] // 2
-        mine = lax.dynamic_slice_in_dim(value, section_index * half, half, split_axis)
-        theirs = lax.dynamic_slice_in_dim(value, (1 - section_index) * half, half, split_axis)
-        summed = mine + swap_sections(theirs.astype(jnp.bfloat16)).astype(jnp.float32)
-        reduced = lax.psum_scatter(
-            summed.astype(jnp.bfloat16), "ctx", scatter_dimension=CTX_AXES[position], tiled=True
-        ).astype(jnp.float32)
-        moved = one_way(reduced, 1 - owner, owner)
-        halves = [reduced, moved] if owner == 0 else [moved, reduced]
-        out[position] = jnp.concatenate(halves, split_axis)
+        total = value + one_way(value.astype(jnp.bfloat16), 1 - owner, owner).astype(jnp.float32)
+        out[position] = owner_scatter(total, owner, axis)
     return tuple(out)
+
+
+def layer_forward(rows, weights, cosine, sine, allowed, score_scale):
+    gains, up_shift, qkv_full, qkv_shift, dense_full, up_full, down_full = weights
+    seq_count, tok_rows, model_width = rows.shape
+    head_count = qkv_full.shape[1]
+    head_dim = qkv_full.shape[2] // 3
+    flat_count = seq_count * tok_rows
+    gain_one, bias_one, gain_two, bias_two, out_shift = (
+        gains[i].astype(jnp.float32) for i in range(5)
+    )
+    up_shift = up_shift.astype(jnp.float32)
+    flat_rows = rows.reshape(flat_count, model_width).astype(jnp.float32)
+    row_mean = jnp.mean(flat_rows, axis=-1, keepdims=True)
+    centered = flat_rows - row_mean
+    row_var = jnp.mean(centered * centered, axis=-1, keepdims=True)
+    inverse = lax.rsqrt(row_var + norm_eps)
+    unit = centered * inverse
+    input_one = (unit * gain_one + bias_one).astype(jnp.bfloat16)
+    input_two = (unit * gain_two + bias_two).astype(jnp.bfloat16)
+    mixed_rows = jnp.dot(
+        input_one, qkv_full.reshape(model_width, -1), preferred_element_type=jnp.float32
+    ) + qkv_shift.astype(jnp.float32).reshape(-1)
+    mixed_rows = mixed_rows.reshape(seq_count, tok_rows, head_count, 3 * head_dim)
+    query_rows = rotate_heads(mixed_rows[..., :head_dim], cosine, sine).astype(jnp.bfloat16)
+    key_rows = rotate_heads(mixed_rows[..., head_dim : 2 * head_dim], cosine, sine).astype(
+        jnp.bfloat16
+    )
+    value_rows = mixed_rows[..., 2 * head_dim :].astype(jnp.bfloat16)
+    key_all, value_all = causal_gather(jnp.stack([key_rows, value_rows]), 2)
+    context, log_total = attend_heads(query_rows, key_all, value_all, allowed, score_scale)
+    pre_act = jnp.dot(input_two, up_full, preferred_element_type=jnp.float32) + up_shift
+    activated, slope = gelu_parts(pre_act)
+    active = activated.astype(jnp.bfloat16)
+    partial_sum = jnp.dot(
+        context.reshape(flat_count, -1), dense_full, preferred_element_type=jnp.float32
+    )
+    partial_sum = partial_sum + jnp.dot(active, down_full, preferred_element_type=jnp.float32)
+    branch = lax.psum(partial_sum.astype(jnp.bfloat16), "tp").astype(jnp.float32)
+    result = (flat_rows + branch + out_shift).reshape(seq_count, tok_rows, model_width)
+    saved = (unit, inverse, input_one, input_two, query_rows, key_all, value_all, context,
+             log_total, slope, active)
+    return result, saved
+
+
+def layer_backward(grad_rows, saved, weights, cosine, sine, allowed, score_scale, tie):
+    gains, _, qkv_full, qkv_shift, dense_full, up_full, down_full = weights
+    (unit, inverse, input_one, input_two, query_rows, key_all, value_all, context, log_total,
+     slope, active) = saved
+    seq_count, tok_rows, model_width = grad_rows.shape
+    head_count = qkv_full.shape[1]
+    head_dim = qkv_full.shape[2] // 3
+    flat_count = seq_count * tok_rows
+    gain_one = gains[0].astype(jnp.float32)
+    gain_two = gains[2].astype(jnp.float32)
+    grad_flat = grad_rows.reshape(flat_count, model_width)
+    grad_half = grad_flat.astype(jnp.bfloat16)
+    grad_out_shift = jnp.sum(grad_flat, 0)
+    grad_down = transposed_dot(active, grad_half)
+    grad_pre = dot_transposed(grad_half, down_full) * slope
+    grad_up_shift = jnp.sum(grad_pre, 0)
+    pre_half = grad_pre.astype(jnp.bfloat16)
+    grad_up = transposed_dot(input_two, pre_half)
+    back_two = dot_transposed(pre_half, up_full)
+    grad_dense = transposed_dot(context.reshape(flat_count, -1), grad_half)
+    grad_context = dot_transposed(grad_half, dense_full).reshape(
+        seq_count, tok_rows, head_count, head_dim
+    )
+    grad_query, grad_key_all, grad_value_all = attend_back(
+        query_rows, key_all, value_all, context, log_total, grad_context, allowed, score_scale
+    )
+    key_value_grads = causal_return(jnp.stack([grad_key_all, grad_value_all]), 2)
+    grad_mixed = jnp.concatenate(
+        [
+            rotate_back(grad_query, cosine, sine),
+            rotate_back(key_value_grads[0], cosine, sine),
+            key_value_grads[1],
+        ],
+        -1,
+    )
+    grad_qkv_shift = jnp.sum(grad_mixed, (0, 1))
+    mixed_half = grad_mixed.reshape(flat_count, -1).astype(jnp.bfloat16)
+    grad_qkv = transposed_dot(input_one, mixed_half).reshape(qkv_full.shape)
+    back_one = dot_transposed(mixed_half, qkv_full.reshape(model_width, -1))
+    norm_terms = jnp.stack(
+        [
+            jnp.sum(back_one * unit, 0),
+            jnp.sum(back_one, 0),
+            jnp.sum(back_two * unit, 0),
+            jnp.sum(back_two, 0),
+        ]
+    )
+    scaled = (back_one * gain_one + back_two * gain_two).astype(jnp.bfloat16)
+    tie, scaled = lax.optimization_barrier((tie, scaled))
+    scaled = lax.psum(scaled, "tp").astype(jnp.float32)
+    first_mean = jnp.mean(scaled, axis=-1, keepdims=True)
+    second_mean = jnp.mean(scaled * unit, axis=-1, keepdims=True)
+    grad_input = grad_flat + inverse * (scaled - first_mean - unit * second_mean)
+    small = jnp.concatenate(
+        [norm_terms, grad_out_shift[None]], 0
+    )
+    grad_terms = (small, grad_qkv, grad_qkv_shift, grad_dense, grad_up, grad_up_shift, grad_down)
+    return grad_input.reshape(seq_count, tok_rows, model_width), grad_terms, tie
 
 
 def on_device(
@@ -333,11 +370,10 @@
     head_dim = w_qkv.shape[3] // 3
     score_scale = 1.0 / math.sqrt(head_dim)
 
-    own = gather_layer(ln1_gain, ln1_bias, ln2_gain, ln2_bias, w_qkv, qkv_bias, w_dense, w_up,
-                       up_bias, w_down, out_bias)
-    other = tuple(swap_sections(piece) for piece in own)
-    first_layer = tuple(jnp.where(section_index == 0, a, b) for a, b in zip(own, other))
-    second_layer = tuple(jnp.where(section_index == 0, b, a) for a, b in zip(own, other))
+    params = (ln1_gain, ln1_bias, ln2_gain, ln2_bias, w_qkv, qkv_bias, w_dense, w_up, up_bias,
+              w_down, out_bias)
+    first_layer = layer_weights(params, 0)
+    second_layer = layer_weights(params, 1)
 
     query_index = context_index * tok_rows + jnp.arange(tok_rows, dtype=jnp.int32)
     allowed = jnp.arange(seq_length, dtype=jnp.int32)[None, :] <= query_index[:, None]

time: 1500 us -> 1510 us (level)
  waiting for transfers between devices: 883 us -> 558 us
  starting transfers between devices: 61.7 us -> 253 us
  local copies, waits for them, and re-layouts: 137 us -> 250 us
  matrix products: 179 us -> 207 us
  other arithmetic: 186 us -> 213 us
  blocking collectives: 25 us -> 0 us
    all_gather x4 -> x0, waiting for transfers between devices: 219 us -> none  [the longest x1 86.5 us: gather_layer(): lax.all_gather(w_down[0], 'ctx', axis=1, tiled=True)]
    reduce_scatter x8 -> x0, waiting for transfers between devices: 212 us -> none  [reduce_layer(): lax.psum_scatter(summed.astype(jnp.bfloat16), 'ctx', scatter_dimension=CT...]
    ppermute x15 -> x54, waiting for transfers between devices: 34.3 us -> 222 us  [the longest x30 112 us: owner_gather(): moved = lax.ppermute(shard, ('section', 'ctx'), section_pairs(owner, shift))]
    ppermute x15 -> x54, starting transfers between devices: 4.45 us -> 140 us  [the longest x30 82.5 us: owner_gather(): moved = lax.ppermute(shard, ('section', 'ctx'), section_pairs(owner, shift))]
    add x0 -> x8, other arithmetic: none -> 84.3 us  [reduce_layer(): value + one_way(value.astype(jnp.bfloat16), 1 - owner, owner).astype(jnp....]
    dynamic_update_slice x0 -> x35, local copies, waits for them, and re-layouts: none -> 67.3 us  [the longest x30 57.7 us: owner_gather(): lax.dynamic_update_slice_in_dim(full, moved, lax.rem(index - shift + coun...]
    psum x2, waiting for transfers between devices: 142 us -> 76.6 us  [layer_backward(): scaled = lax.psum(scaled, 'tp').astype(jnp.float32)]
    ppermute x10 -> x24, starting transfers between devices: 28 us -> 90.3 us  [one_way(): return lax.ppermute(value, 'section', [(src, dst)])]
  transfers between devices with their start and end apart: 55 -> 96, of which waited for: 25 -> 26; matrix products, arithmetic and copies ran while one was open for 24% -> 42% of each run, Pallas kernels for 0% -> 0%
where the time goes in v3:
time: 1510 us; the launch traced here: 1500 us
  waiting for transfers between devices  558 us (37%)
  starting transfers between devices  253 us (17%)
  local copies, waits for them, and re-layouts  250 us (17%)
  other arithmetic  213 us (14%)
  matrix products  207 us (14%)
  between operations  17.3 us (1%)
    psum x2, waiting for transfers between devices, layer_forward(): lax.psum(partial_sum.astype(jnp.bfloat16), 'tp').astype(jnp.float32)  122 us
    ppermute x30, waiting for transfers between devices, owner_gather(): moved = lax.ppermute(shard, ('section', 'ctx'), section_pairs(owner, shift))  112 us
    ppermute x24, waiting for transfers between devices, owner_scatter(): lax.ppermute(piece.astype(jnp.bfloat16), ('section', 'ctx'), section_pair...  110 us
    ppermute x24, starting transfers between devices, one_way(): return lax.ppermute(value, 'section', [(src, dst)])  90.3 us
    add x8, other arithmetic, reduce_layer(): value + one_way(value.astype(jnp.bfloat16), 1 - owner, owner).astype(jnp....  84.3 us
    ppermute x30, starting transfers between devices, owner_gather(): moved = lax.ppermute(shard, ('section', 'ctx'), section_pairs(owner, shift))  82.5 us
    dot_general x8, matrix products, transposed_dot(): lax.dot_general(left, right, (((0,), (0,)), ((), ())), preferred_element_...  76.7 us
    psum x2, waiting for transfers between devices, layer_backward(): scaled = lax.psum(scaled, 'tp').astype(jnp.float32)  76.6 us
  transfers between devices with their start and end apart: 96, of which 26 were waited for; matrix products, arithmetic and copies ran while one was open for 42% of the time, Pallas kernels for 0%

profile of v3, /device:TPU:0, one launch (start us, length us, event | category | flops | bytes accessed | tf_op | source)
XLA Modules:
  0.0 1498.7 jit_solution(13770354077755247958)
XLA Ops:
  88.2 20.3 %collective-permute-start.12 = (bf16[512,512]{1,0:T(8,128)(2,1)S(1)}, bf16[512,512]{1,0:T(8,128)(2,1)S(1)}, u32[]{:S(2)}, u32[]{:S(2)}) collective-permute-start(bf16[512,512]{1,0:T(8,128)(2,1)S(1)} %bitcast.313), channel_id=1, source_target_pairs={{0,4},{4,8},{8,12},{12,0},{1,5},{5,9},{9,13},{13,1},{2,6},{6,10},{... | collective-permute-start | bytes 1572872 | tf_op jit(solution)/shard_map/ppermute | solution.py:162
  182.1 17.1 %collective-permute-done.16 = bf16[512,2048]{1,0:T(8,128)(2,1)} collective-permute-done((bf16[512,2048]{1,0:T(8,128)(2,1)}, bf16[512,2048]{1,0:T(8,128)(2,1)}, u32[]{:S(2)}, u32[]{:S(2)}) %collective-permute-start.16) | collective-permute-done | bytes 2097184 | tf_op jit(solution)/shard_map/ppermute | solution.py:162
  205.5 61.6 %collective-permute-done.17 = bf16[512,2048]{1,0:T(8,128)(2,1)S(1)} collective-permute-done((bf16[512,2048]{1,0:T(8,128)(2,1)}, bf16[512,2048]{1,0:T(8,128)(2,1)S(1)}, u32[]{:S(2)}, u32[]{:S(2)}) %collective-permute-start.17) | collective-permute-done | bytes 2097184 | tf_op jit(solution)/shard_map/ppermute | solution.py:162
  277.2 12.4 collective-permute-done.22
  302.0 10.5 collective-permute-done.23
  390.5 10.2 collective-permute-done.10
  400.7 36.0 %collective-permute-start.15 = (bf16[512,2048]{1,0:T(8,128)(2,1)}, bf16[512,2048]{1,0:T(8,128)(2,1)}, u32[]{:S(2)}, u32[]{:S(2)}) collective-permute-start(bf16[512,2048]{1,0:T(8,128)(2,1)} %constant_dynamic-update-slice_fusion.24), channel_id=1, source_target_pairs={{0,16},{1,17},{2,18},{3,19},{4,20},{5,21},{6,22},{7,23},{8,24},{9,... | collective-permute-start | bytes 6291464 | tf_op jit(solution)/shard_map/ppermute | solution.py:14
  481.9 101.8 %all-reduce.9.cloned.1.call-done = bf16[512,2048]{1,0:T(8,128)(2,1)} async-done(((bf16[512,2048]{1,0:T(8,128)(2,1)}), bf16[512,2048]{1,0:T(8,128)(2,1)}) %all-reduce.9.cloned.1.call-update) | async-done | bytes 2097168 | tf_op jit(solution)/shard_map/psum | solution.py:283
  618.7 10.7 fusion.159
  639.2 10.2 fusion.57
  695.4 20.4 %collective-permute-done.51 = bf16[2,2,256,2,256]{4,2,3,1,0:T(8,128)(2,1)} collective-permute-done((bf16[2,2,256,2,256]{4,2,3,1,0:T(8,128)(2,1)}, bf16[2,2,256,2,256]{4,2,3,1,0:T(8,128)(2,1)}, u32[]{:S(2)}, u32[]{:S(2)}) %collective-permute-start.51) | collective-permute-done | bytes 1048608 | tf_op jit(solution)/shard_map/ppermute | solution.py:41
  741.3 10.4 add_convert_fusion.1
  751.7 20.1 %all-reduce.11.cloned.1.call-done = bf16[512,2048]{1,0:T(8,128)(2,1)} async-done(((bf16[512,2048]{1,0:T(8,128)(2,1)}), bf16[512,2048]{1,0:T(8,128)(2,1)}) %all-reduce.11.cloned.1.call-update) | async-done | bytes 2097168 | tf_op jit(solution)/shard_map/psum | solution.py:283
  776.3 12.7 fusion.157
  818.7 43.2 %all-reduce.13.cloned.1.call-done = bf16[512,2048]{1,0:T(8,128)(2,1)} async-done(((bf16[512,2048]{1,0:T(8,128)(2,1)}), bf16[512,2048]{1,0:T(8,128)(2,1)}) %all-reduce.13.cloned.1.call-update) | async-done | bytes 2097168 | tf_op jit(solution)/shard_map/psum | solution.py:339
  881.3 12.4 fusion.160
  940.8 17.4 %collective-permute-done.54 = bf16[2,2,256,2,256]{4,2,3,1,0:T(8,128)(2,1)} collective-permute-done((bf16[2,2,256,2,256]{4,2,3,1,0:T(8,128)(2,1)}, bf16[2,2,256,2,256]{4,2,3,1,0:T(8,128)(2,1)}, u32[]{:S(2)}, u32[]{:S(2)}) %collective-permute-start.54) | collective-permute-done | bytes 1048608 | tf_op jit(solution)/shard_map/ppermute | solution.py:41
  980.4 11.8 add_convert_fusion
  1006.2 11.0 fusion.158
  1047.2 33.4 %all-reduce.15.cloned.1.call-done = bf16[512,2048]{1,0:T(8,128)(2,1)} async-done(((bf16[512,2048]{1,0:T(8,128)(2,1)}), bf16[512,2048]{1,0:T(8,128)(2,1)}) %all-reduce.15.cloned.1.call-update) | async-done | bytes 2097168 | tf_op jit(solution)/shard_map/psum | solution.py:339
  1093.1 12.3 convert_add_fusion.4
  1106.8 15.7 %convert_add_fusion.2 = f32[2048,2048]{1,0:T(8,128)} fusion(f32[2048,2048]{1,0:T(8,128)} %get-tuple-element.208, bf16[2048,2048]{1,0:T(8,128)(2,1)} %collective-permute-done.78), kind=kLoop, calls=%fused_computation.2 | loop fusion | flops 8388608 | bytes 41943040 | tf_op jit(solution)/shard_map/add | solution.py:242
  1168.3 65.8 %all-reduce.17.cloned.1.call-done = (f32[4,3456]{1,0:T(4,128)}, f32[4,3456]{1,0:T(4,128)}) async-done(((f32[4,3456]{1,0:T(4,128)}, f32[4,3456]{1,0:T(4,128)}), (f32[4,3456]{1,0:T(4,128)}, f32[4,3456]{1,0:T(4,128)})) %all-reduce.17.cloned.1.call-update) | async-done | bytes 110608 | tf_op jit(solution)/shard_map/psum | solution.py:230
  1242.2 12.3 convert_add_fusion.5
  1266.7 14.0 convert_add_fusion.3
  1306.8 14.1 convert_add_fusion.1
  1339.2 27.7 %collective-permute-done.77 = bf16[512,2048]{1,0:T(8,128)(2,1)} collective-permute-done((bf16[512,2048]{1,0:T(8,128)(2,1)}, bf16[512,2048]{1,0:T(8,128)(2,1)}, u32[]{:S(2)}, u32[]{:S(2)}) %collective-permute-start.77) | collective-permute-done | bytes 2097184 | tf_op jit(solution)/shard_map/ppermute | solution.py:178
  1373.3 17.6 %collective-permute-done.75 = bf16[512,2048]{1,0:T(8,128)(2,1)} collective-permute-done((bf16[512,2048]{1,0:T(8,128)(2,1)}, bf16[512,2048]{1,0:T(8,128)(2,1)}, u32[]{:S(2)}, u32[]{:S(2)}) %collective-permute-start.75) | collective-permute-done | bytes 2097184 | tf_op jit(solution)/shard_map/ppermute | solution.py:178
  1412.1 11.6 select_bitcast_fusion.1
  1423.7 10.5 collective-permute-done.85
  1434.2 45.9 %collective-permute-done.84 = bf16[2048,512]{1,0:T(8,128)(2,1)} collective-permute-done((bf16[2048,512]{1,0:T(8,128)(2,1)}, bf16[2048,512]{1,0:T(8,128)(2,1)}, u32[]{:S(2)}, u32[]{:S(2)}) %collective-permute-start.84) | collective-permute-done | bytes 2097184 | tf_op jit(solution)/shard_map/ppermute | solution.py:178
  1480.1 11.3 select_bitcast_fusion
  (685 shorter events, 739.0 us)
Async XLA Ops:
  7.2 576.5 %all-reduce.9.cloned.1.call-start = ((), (), s32[]{:S(2)}) async-start(), calls=%async_computation | async-start | bytes 4194304 | tf_op jit(solution)/shard_map/psum | solution.py:283
  16.4 126.0 %collective-permute-start.4 = (bf16[512,2,768]{2,1,0:T(2,128)(2,1)}, bf16[512,2,768]{2,1,0:T(2,128)(2,1)}, u32[]{:S(2)}, u32[]{:S(2)}) collective-permute-start(bf16[512,2,768]{2,1,0:T(2,128)(2,1)} %bitcast.307), channel_id=1, source_target_pairs={{0,4},{4,8},{8,12},{12,0},{1,5},{5,9},{9,13},{13,1},{2,6},{6,10},{... | collective-permute-start | bytes 4718600 | tf_op jit(solution)/shard_map/ppermute | solution.py:162
  57.9 94.5 %collective-permute-start.5 = (bf16[512,2,768]{2,1,0:T(2,128)(2,1)}, bf16[512,2,768]{2,1,0:T(2,128)(2,1)}, u32[]{:S(2)}, u32[]{:S(2)}) collective-permute-start(bf16[512,2,768]{2,1,0:T(2,128)(2,1)} %bitcast.308), channel_id=1, source_target_pairs={{0,8},{4,12},{8,0},{12,4},{1,9},{5,13},{9,1},{13,5},{2,10},{6,14},... | collective-permute-start | bytes 4718600 | tf_op jit(solution)/shard_map/ppermute | solution.py:162
  59.9 93.9 %collective-permute-start.6 = (bf16[512,2,768]{2,1,0:T(2,128)(2,1)}, bf16[512,2,768]{2,1,0:T(2,128)(2,1)}, u32[]{:S(2)}, u32[]{:S(2)}) collective-permute-start(bf16[512,2,768]{2,1,0:T(2,128)(2,1)} %bitcast.309), channel_id=1, source_target_pairs={{0,12},{4,0},{8,4},{12,8},{1,13},{5,1},{9,5},{13,9},{2,14},{6,2},{... | collective-permute-start | bytes 4718600 | tf_op jit(solution)/shard_map/ppermute | solution.py:162
  165.1 172.7 %collective-permute-start.7 = (bf16[2048,2,768]{2,1,0:T(2,128)(2,1)}, bf16[2048,2,768]{2,1,0:T(2,128)(2,1)}, u32[]{:S(2)}, u32[]{:S(2)}) collective-permute-start(bf16[2048,2,768]{2,1,0:T(2,128)(2,1)} %constant_dynamic-update-slice_fusion.32), channel_id=1, source_target_pairs={{0,16},{1,17},{2,18},{3,19},{4,20},{5,21},{6,22},{7,23},{8,24},{9,... | collective-permute-start | bytes 18874376 | tf_op jit(solution)/shard_map/ppermute | solution.py:14
  173.6 93.5 %collective-permute-start.17 = (bf16[512,2048]{1,0:T(8,128)(2,1)}, bf16[512,2048]{1,0:T(8,128)(2,1)S(1)}, u32[]{:S(2)}, u32[]{:S(2)}) collective-permute-start(bf16[512,2048]{1,0:T(8,128)(2,1)} %bitcast.19), channel_id=1, source_target_pairs={{0,8},{4,12},{8,0},{12,4},{1,9},{5,13},{9,1},{13,5},{2,10},{6,14},... | collective-permute-start | bytes 6291464 | tf_op jit(solution)/shard_map/ppermute | solution.py:162
  177.2 96.7 %collective-permute-start.21 = (bf16[2048,512]{1,0:T(8,128)(2,1)}, bf16[2048,512]{1,0:T(8,128)(2,1)S(1)}, u32[]{:S(2)}, u32[]{:S(2)}) collective-permute-start(bf16[2048,512]{1,0:T(8,128)(2,1)} %bitcast.20), channel_id=1, source_target_pairs={{0,4},{4,8},{8,12},{12,0},{1,5},{5,9},{9,13},{13,1},{2,6},{6,10},{... | collective-permute-start | bytes 6291464 | tf_op jit(solution)/shard_map/ppermute | solution.py:162
  179.7 109.9 %collective-permute-start.22 = (bf16[2048,512]{1,0:T(8,128)(2,1)}, bf16[2048,512]{1,0:T(8,128)(2,1)S(1)}, u32[]{:S(2)}, u32[]{:S(2)}) collective-permute-start(bf16[2048,512]{1,0:T(8,128)(2,1)} %bitcast.20), channel_id=1, source_target_pairs={{0,8},{4,12},{8,0},{12,4},{1,9},{5,13},{9,1},{13,5},{2,10},{6,14},... | collective-permute-start | bytes 6291464 | tf_op jit(solution)/shard_map/ppermute | solution.py:162
  289.6 156.1 %collective-permute-start.19 = (bf16[2048,2048]{1,0:T(8,128)(2,1)}, bf16[2048,2048]{1,0:T(8,128)(2,1)}, u32[]{:S(2)}, u32[]{:S(2)}) collective-permute-start(bf16[2048,2048]{1,0:T(8,128)(2,1)} %constant_dynamic-update-slice_fusion.20), channel_id=1, source_target_pairs={{0,16},{1,17},{2,18},{3,19},{4,20},{5,21},{6,22},{7,23},{8,24},{9,... | collective-permute-start | bytes 25165832 | tf_op jit(solution)/shard_map/ppermute | solution.py:14
  317.4 136.5 %collective-permute-start.24 = (bf16[2048,2048]{1,0:T(8,128)(2,1)}, bf16[2048,2048]{1,0:T(8,128)(2,1)}, u32[]{:S(2)}, u32[]{:S(2)}) collective-permute-start(bf16[2048,2048]{1,0:T(8,128)(2,1)} %constant_dynamic-update-slice_fusion.16), channel_id=1, source_target_pairs={{0,16},{1,17},{2,18},{3,19},{4,20},{5,21},{6,22},{7,23},{8,24},{9,... | collective-permute-start | bytes 25165832 | tf_op jit(solution)/shard_map/ppermute | solution.py:14
  445.7 165.8 %collective-permute-start.44 = (bf16[2048,2048]{1,0:T(8,128)(2,1)}, bf16[2048,2048]{1,0:T(8,128)(2,1)}, u32[]{:S(2)}, u32[]{:S(2)}) collective-permute-start(bf16[2048,2048]{1,0:T(8,128)(2,1)} %constant_dynamic-update-slice_fusion.3), channel_id=1, source_target_pairs={{16,0},{17,1},{18,2},{19,3},{20,4},{21,5},{22,6},{23,7},{24,8},{25... | collective-permute-start | bytes 25165832 | tf_op jit(solution)/shard_map/ppermute | solution.py:14
  467.6 304.1 %all-reduce.11.cloned.1.call-start = ((), (), s32[]{:S(2)}) async-start(), calls=%async_computation.1 | async-start | bytes 4194304 | tf_op jit(solution)/shard_map/psum | solution.py:283
  470.8 158.6 %collective-permute-start.49 = (bf16[2048,2048]{1,0:T(8,128)(2,1)}, bf16[2048,2048]{1,0:T(8,128)(2,1)}, u32[]{:S(2)}, u32[]{:S(2)}) collective-permute-start(bf16[2048,2048]{1,0:T(8,128)(2,1)} %constant_dynamic-update-slice_fusion), channel_id=1, source_target_pairs={{16,0},{17,1},{18,2},{19,3},{20,4},{21,5},{22,6},{23,7},{24,8},{25... | collective-permute-start | bytes 25165832 | tf_op jit(solution)/shard_map/ppermute | solution.py:14
  681.4 180.5 %all-reduce.13.cloned.1.call-start = ((), (), s32[]{:S(2)}) async-start(), calls=%async_computation.2 | async-start | bytes 4194304 | tf_op jit(solution)/shard_map/psum | solution.py:339
  687.0 126.1 %collective-permute-start.70 = (bf16[512,2048]{1,0:T(8,128)(2,1)}, bf16[512,2048]{1,0:T(8,128)(2,1)}, u32[]{:S(2)}, u32[]{:S(2)}) collective-permute-start(bf16[512,2048]{1,0:T(8,128)(2,1)} %get-tuple-element.203), channel_id=1, source_target_pairs={{0,16},{1,17},{2,18},{3,19},{4,20},{5,21},{6,22},{7,23},{8,24},{9,... | collective-permute-start | bytes 6291464 | tf_op jit(solution)/shard_map/ppermute | solution.py:14
  776.2 304.4 %all-reduce.15.cloned.1.call-start = ((), (), s32[]{:S(2)}) async-start(), calls=%async_computation.3 | async-start | bytes 4194304 | tf_op jit(solution)/shard_map/psum | solution.py:339
  789.6 315.8 %collective-permute-start.78 = (bf16[2048,2048]{1,0:T(8,128)(2,1)}, bf16[2048,2048]{1,0:T(8,128)(2,1)}, u32[]{:S(2)}, u32[]{:S(2)}) collective-permute-start(bf16[2048,2048]{1,0:T(8,128)(2,1)} %get-tuple-element.207), channel_id=1, source_target_pairs={{0,16},{1,17},{2,18},{3,19},{4,20},{5,21},{6,22},{7,23},{8,24},{9,... | collective-permute-start | bytes 25165832 | tf_op jit(solution)/shard_map/ppermute | solution.py:14
  794.6 334.6 %collective-permute-start.86 = (bf16[2048,2048]{1,0:T(8,128)(2,1)}, bf16[2048,2048]{1,0:T(8,128)(2,1)}, u32[]{:S(2)}, u32[]{:S(2)}) collective-permute-start(bf16[2048,2048]{1,0:T(8,128)(2,1)} %get-tuple-element.211), channel_id=1, source_target_pairs={{0,16},{1,17},{2,18},{3,19},{4,20},{5,21},{6,22},{7,23},{8,24},{9,... | collective-permute-start | bytes 25165832 | tf_op jit(solution)/shard_map/ppermute | solution.py:14
  936.9 154.9 %collective-permute-start.62 = (bf16[2048,2,768]{2,0,1:T(8,128)(2,1)}, bf16[2048,2,768]{2,0,1:T(8,128)(2,1)}, u32[]{:S(2)}, u32[]{:S(2)}) collective-permute-start(bf16[2048,2,768]{2,0,1:T(8,128)(2,1)} %get-tuple-element.199), channel_id=1, source_target_pairs={{0,16},{1,17},{2,18},{3,19},{4,20},{5,21},{6,22},{7,23},{8,24},{9,... | collective-permute-start | bytes 18874376 | tf_op jit(solution)/shard_map/ppermute | solution.py:14
  992.3 159.4 %all-reduce.19.cloned.1.call-start = ((), (), s32[]{:S(2)}) async-start(), calls=%async_computation.5 | async-start | bytes 131072 | tf_op jit(solution)/shard_map/psum | solution.py:221
  1038.8 102.4 %collective-permute-start.57 = (f32[2,256,2048]{2,1,0:T(8,128)}, f32[2,256,2048]{2,1,0:T(8,128)}, u32[]{:S(2)}, u32[]{:S(2)}) collective-permute-start(f32[2,256,2048]{2,1,0:T(8,128)} %bitcast.37), channel_id=1, source_target_pairs={{0,16},{1,17},{2,18},{3,19},{4,20},{5,21},{6,22},{7,23},{8,24},{9,... | collective-permute-start | bytes 12582920 | tf_op jit(solution)/shard_map/ppermute | solution.py:14
  1042.1 220.2 %collective-permute-start.74 = (bf16[2048,2048]{1,0:T(8,128)(2,1)}, bf16[2048,2048]{1,0:T(8,128)(2,1)}, u32[]{:S(2)}, u32[]{:S(2)}) collective-permute-start(bf16[2048,2048]{1,0:T(8,128)(2,1)} %get-tuple-element.209), channel_id=1, source_target_pairs={{16,0},{17,1},{18,2},{19,3},{20,4},{21,5},{22,6},{23,7},{24,8},{25... | collective-permute-start | bytes 25165832 | tf_op jit(solution)/shard_map/ppermute | solution.py:14
  1086.9 147.3 %all-reduce.17.cloned.1.call-start = ((), (), s32[]{:S(2)}) async-start(), calls=%async_computation.4 | async-start | bytes 221184 | tf_op jit(solution)/shard_map/psum | solution.py:230
  1105.4 192.9 %collective-permute-start.82 = (bf16[2048,2048]{1,0:T(8,128)(2,1)}, bf16[2048,2048]{1,0:T(8,128)(2,1)}, u32[]{:S(2)}, u32[]{:S(2)}) collective-permute-start(bf16[2048,2048]{1,0:T(8,128)(2,1)} %get-tuple-element.213), channel_id=1, source_target_pairs={{16,0},{17,1},{18,2},{19,3},{20,4},{21,5},{22,6},{23,7},{24,8},{25... | collective-permute-start | bytes 25165832 | tf_op jit(solution)/shard_map/ppermute | solution.py:14
  1156.4 137.7 %collective-permute-start.56 = (f32[2,256,2048]{2,1,0:T(8,128)}, f32[2,256,2048]{2,1,0:T(8,128)}, u32[]{:S(2)}, u32[]{:S(2)}) collective-permute-start(f32[2,256,2048]{2,1,0:T(8,128)} %bitcast.282), channel_id=1, source_target_pairs={{16,0},{17,1},{18,2},{19,3},{20,4},{21,5},{22,6},{23,7},{24,8},{25... | collective-permute-start | bytes 12582920 | tf_op jit(solution)/shard_map/ppermute | solution.py:14
  1157.8 103.0 %collective-permute-start.81 = (bf16[512,2048]{1,0:T(8,128)(2,1)}, bf16[512,2048]{1,0:T(8,128)(2,1)S(1)}, u32[]{:S(2)}, u32[]{:S(2)}) collective-permute-start(bf16[512,2048]{1,0:T(8,128)(2,1)} %get-tuple-element.102), channel_id=1, source_target_pairs={{16,28},{20,16},{24,20},{28,24},{17,29},{21,17},{25,21},{29,25},{1... | collective-permute-start | bytes 6291464 | tf_op jit(solution)/shard_map/ppermute | solution.py:178
  1158.6 103.0 %collective-permute-start.80 = (bf16[512,2048]{1,0:T(8,128)(2,1)}, bf16[512,2048]{1,0:T(8,128)(2,1)}, u32[]{:S(2)}, u32[]{:S(2)}) collective-permute-start(bf16[512,2048]{1,0:T(8,128)(2,1)} %get-tuple-element.103), channel_id=1, source_target_pairs={{16,24},{20,28},{24,16},{28,20},{17,25},{21,29},{25,17},{29,21},{1... | collective-permute-start | bytes 6291464 | tf_op jit(solution)/shard_map/ppermute | solution.py:178
  1301.9 89.0 %collective-permute-start.75 = (bf16[512,2048]{1,0:T(8,128)(2,1)}, bf16[512,2048]{1,0:T(8,128)(2,1)}, u32[]{:S(2)}, u32[]{:S(2)}) collective-permute-start(bf16[512,2048]{1,0:T(8,128)(2,1)} %get-tuple-element.98), channel_id=1, source_target_pairs={{0,4},{4,8},{8,12},{12,0},{1,5},{5,9},{9,13},{13,1},{2,6},{6,10},{... | collective-permute-start | bytes 6291464 | tf_op jit(solution)/shard_map/ppermute | solution.py:178
  1332.6 91.0 %collective-permute-start.88 = (bf16[2048,512]{1,0:T(8,128)(2,1)}, bf16[2048,512]{1,0:T(8,128)(2,1)}, u32[]{:S(2)}, u32[]{:S(2)}) collective-permute-start(bf16[2048,512]{1,0:T(8,128)(2,1)} %get-tuple-element.97), channel_id=1, source_target_pairs={{16,24},{20,28},{24,16},{28,20},{17,25},{21,29},{25,17},{29,21},{1... | collective-permute-start | bytes 6291464 | tf_op jit(solution)/shard_map/ppermute | solution.py:178
  1337.3 86.4 %collective-permute-start.87 = (bf16[2048,512]{1,0:T(8,128)(2,1)S(1)}, bf16[2048,512]{1,0:T(8,128)(2,1)}, u32[]{:S(2)}, u32[]{:S(2)}) collective-permute-start(bf16[2048,512]{1,0:T(8,128)(2,1)S(1)} %copy-done.43), channel_id=1, source_target_pairs={{16,20},{20,24},{24,28},{28,16},{17,21},{21,25},{25,29},{29,17},{1... | collective-permute-start | bytes 6291464 | tf_op jit(solution)/shard_map/ppermute | solution.py:178
  1370.5 109.6 %collective-permute-start.84 = (bf16[2048,512]{1,0:T(8,128)(2,1)}, bf16[2048,512]{1,0:T(8,128)(2,1)}, u32[]{:S(2)}, u32[]{:S(2)}) collective-permute-start(bf16[2048,512]{1,0:T(8,128)(2,1)} %get-tuple-element.94), channel_id=1, source_target_pairs={{0,8},{4,12},{8,0},{12,4},{1,9},{5,13},{9,1},{13,5},{2,10},{6,14},... | collective-permute-start | bytes 6291464 | tf_op jit(solution)/shard_map/ppermute | solution.py:178
  1390.9 89.2 %collective-permute-start.83 = (bf16[2048,512]{1,0:T(8,128)(2,1)}, bf16[2048,512]{1,0:T(8,128)(2,1)}, u32[]{:S(2)}, u32[]{:S(2)}) collective-permute-start(bf16[2048,512]{1,0:T(8,128)(2,1)} %get-tuple-element.92), channel_id=1, source_target_pairs={{0,4},{4,8},{8,12},{12,0},{1,5},{5,9},{9,13},{13,1},{2,6},{6,10},{... | collective-permute-start | bytes 6291464 | tf_op jit(solution)/shard_map/ppermute | solution.py:178
  (190 other events, 4793.2 us)
Sparse Core Ops, SparseCore 0:
  467.8 115.9 all-reduce.8
  681.5 90.2 all-reduce.10
  776.4 85.4 all-reduce.12
  992.4 88.1 all-reduce.14
  1087.0 33.0 all-reduce.18
  1156.5 77.5 all-reduce.16

commit v4 on v2

--- a/solution.py
+++ b/solution.py
@@ -355,8 +355,8 @@
     )
     top_other = one_way(top, 0, 1)
     reduced_second = reduce_layer(terms_second, 1)
-    grad_in, terms_first, _ = layer_backward(
-        grad_mid, saved_first, first_layer, cosine, sine, allowed, score_scale, grad_mid
+    grad_in, terms_first, reduced_second = layer_backward(
+        grad_mid, saved_first, first_layer, cosine, sine, allowed, score_scale, reduced_second
     )
     reduced_first = reduce_layer(terms_first, 0)
     grad_other = one_way(grad_in, 1, 0)

time: 1500 us -> 1350 us (0.900)
  waiting for transfers between devices: 883 us -> 618 us
  blocking collectives: 25 us -> 124 us
  local copies, waits for them, and re-layouts: 137 us -> 162 us
    reduce_scatter x8, waiting for transfers between devices: 212 us -> 116 us  [reduce_layer(): lax.psum_scatter(summed.astype(jnp.bfloat16), 'ctx', scatter_dimension=CT...]
    psum x0 -> x4, blocking collectives: none -> 95.4 us  [the longest x2 59.2 us: reduce_layer(): packed = lax.psum(jnp.concatenate(flat, 1), ('section', 'ctx'))]
    psum x2, waiting for transfers between devices: 142 us -> 63.9 us  [layer_backward(): scaled = lax.psum(scaled, 'tp').astype(jnp.float32)]
    psum x2 -> x0, waiting for transfers between devices: 55.1 us -> none  [the longest x1 55.1 us: reduce_layer(): packed = lax.psum(jnp.concatenate(flat, 1), ('section', 'ctx'))]
    ppermute x6, waiting for transfers between devices: 57.4 us -> 37 us  [causal_gather(): lax.ppermute(block, 'ctx', [(i, i + shift) for i in range(count - shift)])]
    psum x2, waiting for transfers between devices: 99 us -> 81.4 us  [layer_forward(): lax.psum(partial_sum.astype(jnp.bfloat16), 'tp').astype(jnp.float32)]
    broadcast_in_dim x0 -> x5, other arithmetic: none -> 17.1 us  [the longest x1 5.48 us: on_device(): g_up[None]]
    select_n x8 -> x3, other arithmetic: 31 us -> 14.5 us  [on_device(): jnp.where(section_index == 0, a, b)]
  transfers between devices with their start and end apart: 55 -> 53, of which waited for: 25 -> 21; matrix products, arithmetic and copies ran while one was open for 24% -> 34% of each run, Pallas kernels for 0% -> 0%
where the time goes in v4:
time: 1350 us; the launch traced here: 1340 us
  waiting for transfers between devices  618 us (46%)
  other arithmetic  187 us (14%)
  matrix products  185 us (14%)
  local copies, waits for them, and re-layouts  162 us (12%)
  blocking collectives  124 us (9%)
  starting transfers between devices  49.1 us (4%)
  between operations  16.3 us (1%)
    reduce_scatter x8, waiting for transfers between devices, reduce_layer(): lax.psum_scatter(summed.astype(jnp.bfloat16), 'ctx', scatter_dimension=CT...  116 us
    all_gather x1, waiting for transfers between devices, gather_layer(): lax.all_gather(w_down[0], 'ctx', axis=1, tiled=True)  86.5 us
    unnamed x224, local copies, waits for them, and re-layouts  82.5 us
    psum x2, waiting for transfers between devices, layer_forward(): lax.psum(partial_sum.astype(jnp.bfloat16), 'tp').astype(jnp.float32)  81.4 us
    ppermute x6, waiting for transfers between devices, causal_return(): lax.ppermute(piece.astype(jnp.bfloat16), 'ctx', [(i + shift, i) for i in...  75.1 us
    all_gather x1, waiting for transfers between devices, gather_layer(): lax.all_gather(w_qkv[0], 'ctx', axis=0, tiled=True)  73.3 us
    dot_general x8, matrix products, dot_transposed(): lax.dot_general(left, right, (((1,), (1,)), ((), ())), preferred_element_...  66.2 us
    psum x2, waiting for transfers between devices, layer_backward(): scaled = lax.psum(scaled, 'tp').astype(jnp.float32)  63.9 us
  transfers between devices with their start and end apart: 53, of which 21 were waited for; matrix products, arithmetic and copies ran while one was open for 34% of the time, Pallas kernels for 0%

profile of v4, /device:TPU:0, one launch (start us, length us, event | category | flops | bytes accessed | tf_op | source)
XLA Modules:
  0.0 1341.3 jit_solution(4910194792410742730)
XLA Ops:
  9.5 73.3 %all-gather.11.cloned.1.call-done = bf16[1,2048,2,768]{3,2,0,1:T(2,128)(2,1)} async-done(((bf16[1,512,2,768]{3,2,0,1:T(2,128)(2,1)}), bf16[1,2048,2,768]{3,2,0,1:T(2,128)(2,1)}) %all-gather.11.cloned.1.call-update) | async-done | bytes 6291472 | tf_op jit(solution)/shard_map/all_gather | solution.py:158
  82.8 8.0 all-gather.4
  98.5 13.8 %all-gather.1 = bf16[1,2,768]{1,0,2:T(2,128)(2,1)S(1)} all-gather(bf16[1,2,192]{1,0,2:T(2,128)(2,1)S(1)} %copy.241), channel_id=3, replica_groups=mesh['section'=2,'ctx'=4,'tp'=4] {'ctx'}, dimensions={2}, use_global_device_ids=true | all-gather | bytes 3840 | tf_op jit(solution)/shard_map/all_gather | solution.py:159
  117.1 58.5 %all-gather.15.cloned.1.call-done = bf16[1,2048,2048]{2,1,0:T(8,128)(2,1)} async-done(((bf16[1,512,2048]{2,1,0:T(8,128)(2,1)}), bf16[1,2048,2048]{2,1,0:T(8,128)(2,1)}) %all-gather.15.cloned.1.call-update) | async-done | bytes 8388624 | tf_op jit(solution)/shard_map/all_gather | solution.py:161
  178.3 86.5 %all-gather.17.cloned.1.call-done = bf16[1,2048,2048]{2,1,0:T(8,128)(2,1)} async-done(((bf16[1,2048,512]{2,1,0:T(8,128)(2,1)}), bf16[1,2048,2048]{2,1,0:T(8,128)(2,1)}) %all-gather.17.cloned.1.call-update) | async-done | bytes 8388624 | tf_op jit(solution)/shard_map/all_gather | solution.py:162
  264.9 12.9 broadcast_select_fusion.1
  312.5 14.5 %collective-permute-done.3 = bf16[2,2,256,2,256]{4,2,3,1,0:T(8,128)(2,1)} collective-permute-done((bf16[2,2,256,2,256]{4,2,3,1,0:T(8,128)(2,1)}, bf16[2,2,256,2,256]{4,2,3,1,0:T(8,128)(2,1)}, u32[]{:S(2)}, u32[]{:S(2)}) %collective-permute-start.3) | collective-permute-done | bytes 1048608 | tf_op jit(solution)/shard_map/ppermute | solution.py:29
  328.7 22.5 %collective-permute-done.4 = bf16[2,2,256,2,256]{4,2,3,1,0:T(8,128)(2,1)} collective-permute-done((bf16[2,2,256,2,256]{4,2,3,1,0:T(8,128)(2,1)}, bf16[2,2,256,2,256]{4,2,3,1,0:T(8,128)(2,1)}, u32[]{:S(2)}, u32[]{:S(2)}) %collective-permute-start.4) | collective-permute-done | bytes 1048608 | tf_op jit(solution)/shard_map/ppermute | solution.py:29
  359.7 10.8 fusion.55
  399.5 74.2 %all-reduce.5.cloned.1.call-done = bf16[512,2048]{1,0:T(8,128)(2,1)} async-done(((bf16[512,2048]{1,0:T(8,128)(2,1)}), bf16[512,2048]{1,0:T(8,128)(2,1)}) %all-reduce.5.cloned.1.call-update) | async-done | bytes 2097168 | tf_op jit(solution)/shard_map/psum | solution.py:202
  499.9 9.8 fusion.58
  525.5 12.2 fusion.166
  537.8 12.4 fusion.59
  592.7 8.2 collective-permute-done.13
  600.9 23.8 %collective-permute-done.14 = bf16[2,2,256,2,256]{4,2,3,1,0:T(8,128)(2,1)} collective-permute-done((bf16[2,2,256,2,256]{4,2,3,1,0:T(8,128)(2,1)}, bf16[2,2,256,2,256]{4,2,3,1,0:T(8,128)(2,1)}, u32[]{:S(2)}, u32[]{:S(2)}) %collective-permute-start.14) | collective-permute-done | bytes 1048608 | tf_op jit(solution)/shard_map/ppermute | solution.py:41
  653.4 12.8 add_convert_fusion.7
  677.8 8.5 add_convert_fusion.2
  736.0 8.3 add_convert_fusion.3
  745.4 47.2 %all-reduce.9.cloned.1.call-done = bf16[512,2048]{1,0:T(8,128)(2,1)} async-done(((bf16[512,2048]{1,0:T(8,128)(2,1)}), bf16[512,2048]{1,0:T(8,128)(2,1)}) %all-reduce.9.cloned.1.call-update) | async-done | bytes 2097168 | tf_op jit(solution)/shard_map/psum | solution.py:258
  810.4 17.1 %psum.59 = f32[4,2048]{1,0:T(4,128)S(1)} all-reduce(f32[4,2048]{1,0:T(4,128)S(1)} %pad_maximum_fusion.16), channel_id=1, replica_groups=mesh['section'=2,'ctx'=4,'tp'=4] {'tp'}, use_global_device_ids=true, to_apply=%region_18.19 | all-reduce | flops 8192 | bytes 65536 | tf_op jit(solution)/shard_map/psum | solution.py:278
  839.7 28.9 %psum.60 = f32[4,3456]{1,0:T(4,128)S(1)} all-reduce(f32[4,3456]{1,0:T(4,128)S(1)} %pad_maximum_fusion.14), channel_id=1, replica_groups=mesh['section'=2,'ctx'=4,'tp'=4] {'section','ctx'}, use_global_device_ids=true, to_apply=%region_22.23 | all-reduce | flops 13824 | bytes 110592 | tf_op jit(solution)/shard_map/psum | solution.py:287
  886.5 10.9 fusion.167
  897.4 15.6 %collective-permute-done.24 = bf16[2,2,256,2,256]{4,2,3,1,0:T(8,128)(2,1)S(1)} collective-permute-done((bf16[2,2,256,2,256]{4,2,3,1,0:T(8,128)(2,1)S(1)}, bf16[2,2,256,2,256]{4,2,3,1,0:T(8,128)(2,1)S(1)}, u32[]{:S(2)}, u32[]{:S(2)}) %collective-permute-start.24) | collective-permute-done | bytes 1048608 | tf_op jit(solution)/shard_map/ppermute | solution.py:41
  913.0 24.4 %collective-permute-done.25 = bf16[2,2,256,2,256]{4,2,3,1,0:T(8,128)(2,1)S(1)} collective-permute-done((bf16[2,2,256,2,256]{4,2,3,1,0:T(8,128)(2,1)S(1)}, bf16[2,2,256,2,256]{4,2,3,1,0:T(8,128)(2,1)S(1)}, u32[]{:S(2)}, u32[]{:S(2)}) %collective-permute-start.25) | collective-permute-done | bytes 1048608 | tf_op jit(solution)/shard_map/ppermute | solution.py:41
  988.9 12.7 add_convert_fusion.6
  1081.8 16.8 %all-reduce.11.cloned.1.call-done = bf16[512,2048]{1,0:T(8,128)(2,1)} async-done(((bf16[512,2048]{1,0:T(8,128)(2,1)}), bf16[512,2048]{1,0:T(8,128)(2,1)}) %all-reduce.11.cloned.1.call-update) | async-done | bytes 2097168 | tf_op jit(solution)/shard_map/psum | solution.py:258
  1112.3 32.1 %reduce-scatter.17.cloned.1.call-done = bf16[512,2,384]{2,0,1:T(8,128)(2,1)} async-done(((bf16[2048,2,384]{2,0,1:T(8,128)(2,1)}), bf16[512,2,384]{2,0,1:T(8,128)(2,1)}) %reduce-scatter.17.cloned.1.call-update) | async-done | bytes 786448 | tf_op jit(solution)/shard_map/reduce_scatter | solution.py:304
  1148.2 51.7 %reduce-scatter.23.cloned.1.call-done = bf16[1024,512]{1,0:T(8,128)(2,1)} async-done(((bf16[1024,2048]{1,0:T(8,128)(2,1)}), bf16[1024,512]{1,0:T(8,128)(2,1)}) %reduce-scatter.23.cloned.1.call-update) | async-done | bytes 1048592 | tf_op jit(solution)/shard_map/reduce_scatter | solution.py:304
  1204.0 19.0 %psum.62 = f32[4,2048]{1,0:T(4,128)S(1)} all-reduce(f32[4,2048]{1,0:T(4,128)S(1)} %pad_maximum_fusion.17), channel_id=1, replica_groups=mesh['section'=2,'ctx'=4,'tp'=4] {'tp'}, use_global_device_ids=true, to_apply=%region_35.36 | all-reduce | flops 8192 | bytes 65536 | tf_op jit(solution)/shard_map/psum | solution.py:278
  1224.0 32.3 %reduce-scatter.21.cloned.1.call-done = bf16[512,1024]{1,0:T(8,128)(2,1)} async-done(((bf16[2048,1024]{1,0:T(8,128)(2,1)}), bf16[512,1024]{1,0:T(8,128)(2,1)}) %reduce-scatter.21.cloned.1.call-update) | async-done | bytes 1048592 | tf_op jit(solution)/shard_map/reduce_scatter | solution.py:304
  1261.7 30.4 %psum.63 = f32[4,3456]{1,0:T(4,128)} all-reduce(f32[4,3456]{1,0:T(4,128)} %pad_maximum_fusion.15), channel_id=1, replica_groups=mesh['section'=2,'ctx'=4,'tp'=4] {'section','ctx'}, use_global_device_ids=true, to_apply=%region_39.40 | all-reduce | flops 13824 | bytes 110592 | tf_op jit(solution)/shard_map/psum | solution.py:287
  1326.6 7.8 maximum_select_fusion
  (525 shorter events, 507.4 us)
Async XLA Ops:
  7.2 75.6 %all-gather.11.cloned.1.call-start = ((), (), s32[]{:S(2)}) async-start(), calls=%async_computation.20 | async-start | bytes 7864320 | tf_op jit(solution)/shard_map/all_gather | solution.py:158
  8.0 167.6 %all-gather.15.cloned.1.call-start = ((), (), s32[]{:S(2)}) async-start(), calls=%async_computation.22 | async-start | bytes 10485760 | tf_op jit(solution)/shard_map/all_gather | solution.py:161
  8.7 256.2 %all-gather.17.cloned.1.call-start = ((), (), s32[]{:S(2)}) async-start(), calls=%async_computation.23 | async-start | bytes 10485760 | tf_op jit(solution)/shard_map/all_gather | solution.py:162
  9.5 303.0 %all-gather.13.cloned.1.call-start = ((), (), s32[]{:S(2)}) async-start(), calls=%async_computation.21 | async-start | bytes 2621440 | tf_op jit(solution)/shard_map/all_gather | solution.py:160
  82.8 182.1 %collective-permute-start.1 = (bf16[2048,2,768]{2,1,0:T(2,128)(2,1)}, bf16[2048,2,768]{2,1,0:T(2,128)(2,1)}, u32[]{:S(2)}, u32[]{:S(2)}) collective-permute-start(bf16[2048,2,768]{2,1,0:T(2,128)(2,1)} %bitcast.334), channel_id=1, source_target_pairs={{0,16},{16,0},{1,17},{17,1},{2,18},{18,2},{3,19},{19,3},{4,20},{20... | collective-permute-start | bytes 18874376 | tf_op jit(solution)/shard_map/ppermute | solution.py:18
  90.9 216.4 %collective-permute-start.8 = (bf16[2048]{0:T(1024)(128)(2,1)S(1)}, bf16[2048]{0:T(1024)(128)(2,1)S(1)}, u32[]{:S(2)}, u32[]{:S(2)}) collective-permute-start(bf16[2048]{0:T(1024)(128)(2,1)S(1)} %reduce.3), channel_id=1, source_target_pairs={{0,16},{16,0},{1,17},{17,1},{2,18},{18,2},{3,19},{19,3},{4,20},{20... | collective-permute-start | bytes 12296 | tf_op jit(solution)/shard_map/ppermute | solution.py:18
  112.6 361.0 %all-reduce.5.cloned.1.call-start = ((), (), s32[]{:S(2)}) async-start(), calls=%async_computation.8 | async-start | bytes 4194304 | tf_op jit(solution)/shard_map/psum | solution.py:202
  175.6 184.1 %collective-permute-start.7 = (bf16[2048,2048]{1,0:T(8,128)(2,1)}, bf16[2048,2048]{1,0:T(8,128)(2,1)}, u32[]{:S(2)}, u32[]{:S(2)}) collective-permute-start(bf16[2048,2048]{1,0:T(8,128)(2,1)} %bitcast.385), channel_id=1, source_target_pairs={{0,16},{16,0},{1,17},{17,1},{2,18},{18,2},{3,19},{19,3},{4,20},{20... | collective-permute-start | bytes 25165832 | tf_op jit(solution)/shard_map/ppermute | solution.py:18
  264.9 105.6 %collective-permute-start.9 = (bf16[2048,2048]{1,0:T(8,128)(2,1)}, bf16[2048,2048]{1,0:T(8,128)(2,1)}, u32[]{:S(2)}, u32[]{:S(2)}) collective-permute-start(bf16[2048,2048]{1,0:T(8,128)(2,1)} %bitcast.388), channel_id=1, source_target_pairs={{0,16},{16,0},{1,17},{17,1},{2,18},{18,2},{3,19},{19,3},{4,20},{20... | collective-permute-start | bytes 25165832 | tf_op jit(solution)/shard_map/ppermute | solution.py:18
  380.2 293.2 %all-reduce.7.cloned.1.call-start = ((), (), s32[]{:S(2)}) async-start(), calls=%async_computation.9 | async-start | bytes 4194304 | tf_op jit(solution)/shard_map/psum | solution.py:202
  490.4 63.7 %collective-permute-start.12 = (bf16[2,2,256,2,256]{4,2,3,1,0:T(8,128)(2,1)}, bf16[2,2,256,2,256]{4,2,3,1,0:T(8,128)(2,1)}, u32[]{:S(2)}, u32[]{:S(2)}) collective-permute-start(bf16[2,2,256,2,256]{4,2,3,1,0:T(8,128)(2,1)} %pad_maximum_fusion.4), channel_id=1, source_target_pairs={{0,4},{4,8},{8,12},{1,5},{5,9},{9,13},{2,6},{6,10},{10,14},{3,7},{... | collective-permute-start | bytes 3145736 | tf_op jit(solution)/shard_map/ppermute | solution.py:29
  494.9 57.9 %collective-permute-start.11 = (bf16[2,2,256,2,256]{4,2,3,1,0:T(8,128)(2,1)}, bf16[2,2,256,2,256]{4,2,3,1,0:T(8,128)(2,1)}, u32[]{:S(2)}, u32[]{:S(2)}) collective-permute-start(bf16[2,2,256,2,256]{4,2,3,1,0:T(8,128)(2,1)} %pad_maximum_fusion.4), channel_id=1, source_target_pairs={{0,8},{4,12},{1,9},{5,13},{2,10},{6,14},{3,11},{7,15},{16,24},{20,... | collective-permute-start | bytes 3145736 | tf_op jit(solution)/shard_map/ppermute | solution.py:29
  498.3 51.8 %collective-permute-start.10 = (bf16[2,2,256,2,256]{4,2,3,1,0:T(8,128)(2,1)}, bf16[2,2,256,2,256]{4,2,3,1,0:T(8,128)(2,1)S(1)}, u32[]{:S(2)}, u32[]{:S(2)}) collective-permute-start(bf16[2,2,256,2,256]{4,2,3,1,0:T(8,128)(2,1)} %pad_maximum_fusion.4), channel_id=1, source_target_pairs={{0,12},{1,13},{2,14},{3,15},{16,28},{17,29},{18,30},{19,31}} | collective-permute-start | bytes 3145736 | tf_op jit(solution)/shard_map/ppermute | solution.py:29
  525.5 152.3 %collective-permute-start.22 = (bf16[1024,2048]{1,0:T(8,128)(2,1)}, bf16[1024,2048]{1,0:T(8,128)(2,1)}, u32[]{:S(2)}, u32[]{:S(2)}) collective-permute-start(bf16[1024,2048]{1,0:T(8,128)(2,1)} %dynamic-slice_convert_fusion.2), channel_id=1, source_target_pairs={{0,16},{16,0},{1,17},{17,1},{2,18},{18,2},{3,19},{19,3},{4,20},{20... | collective-permute-start | bytes 12582920 | tf_op jit(solution)/shard_map/ppermute | solution.py:18
  583.5 145.6 %reduce-scatter.11.cloned.1.call-start = ((), (), s32[]{:S(2)}) async-start(), calls=%async_computation.12 | async-start | bytes 1310720 | tf_op jit(solution)/shard_map/reduce_scatter | solution.py:304
  645.1 147.5 %all-reduce.9.cloned.1.call-start = ((), (), s32[]{:S(2)}) async-start(), calls=%async_computation.10 | async-start | bytes 4194304 | tf_op jit(solution)/shard_map/psum | solution.py:258
  677.8 294.7 %reduce-scatter.15.cloned.1.call-start = ((), (), s32[]{:S(2)}) async-start(), calls=%async_computation.14 | async-start | bytes 5242880 | tf_op jit(solution)/shard_map/reduce_scatter | solution.py:304
  686.4 294.7 %reduce-scatter.9.cloned.1.call-start = ((), (), s32[]{:S(2)}) async-start(), calls=%async_computation.11 | async-start | bytes 3932160 | tf_op jit(solution)/shard_map/reduce_scatter | solution.py:304
  713.5 272.4 %reduce-scatter.13.cloned.1.call-start = ((), (), s32[]{:S(2)}) async-start(), calls=%async_computation.13 | async-start | bytes 5242880 | tf_op jit(solution)/shard_map/reduce_scatter | solution.py:304
  744.3 334.3 %reduce-scatter.19.cloned.1.call-start = ((), (), s32[]{:S(2)}) async-start(), calls=%async_computation.17 | async-start | bytes 1310720 | tf_op jit(solution)/shard_map/reduce_scatter | solution.py:304
  879.4 58.0 %collective-permute-start.25 = (bf16[2,2,256,2,256]{4,2,3,1,0:T(8,128)(2,1)S(1)}, bf16[2,2,256,2,256]{4,2,3,1,0:T(8,128)(2,1)S(1)}, u32[]{:S(2)}, u32[]{:S(2)}) collective-permute-start(bf16[2,2,256,2,256]{4,2,3,1,0:T(8,128)(2,1)S(1)} %get-tuple-element.119), channel_id=1, source_target_pairs={{8,0},{12,4},{9,1},{13,5},{10,2},{14,6},{11,3},{15,7},{24,16},{28,... | collective-permute-start | bytes 3145736 | tf_op jit(solution)/shard_map/ppermute | solution.py:41
  880.8 59.8 %collective-permute-start.26 = (bf16[2,2,256,2,256]{4,2,3,1,0:T(8,128)(2,1)S(1)}, bf16[2,2,256,2,256]{4,2,3,1,0:T(8,128)(2,1)S(1)}, u32[]{:S(2)}, u32[]{:S(2)}) collective-permute-start(bf16[2,2,256,2,256]{4,2,3,1,0:T(8,128)(2,1)S(1)} %get-tuple-element.120), channel_id=1, source_target_pairs={{12,0},{13,1},{14,2},{15,3},{28,16},{29,17},{30,18},{31,19}} | collective-permute-start | bytes 3145736 | tf_op jit(solution)/shard_map/ppermute | solution.py:41
  886.5 91.3 %collective-permute-start.31 = (bf16[256,2048]{1,0:T(8,128)(2,1)}, bf16[256,2048]{1,0:T(8,128)(2,1)}, u32[]{:S(2)}, u32[]{:S(2)}) collective-permute-start(bf16[256,2048]{1,0:T(8,128)(2,1)} %dynamic-slice_convert_fusion.6), channel_id=1, source_target_pairs={{0,16},{16,0},{1,17},{17,1},{2,18},{18,2},{3,19},{19,3},{4,20},{20... | collective-permute-start | bytes 3145736 | tf_op jit(solution)/shard_map/ppermute | solution.py:18
  981.0 117.6 %all-reduce.11.cloned.1.call-start = ((), (), s32[]{:S(2)}) async-start(), calls=%async_computation.15 | async-start | bytes 4194304 | tf_op jit(solution)/shard_map/psum | solution.py:258
  1012.0 132.4 %reduce-scatter.17.cloned.1.call-start = ((), (), s32[]{:S(2)}) async-start(), calls=%async_computation.16 | async-start | bytes 3932160 | tf_op jit(solution)/shard_map/reduce_scatter | solution.py:304
  1018.3 181.6 %reduce-scatter.23.cloned.1.call-start = ((), (), s32[]{:S(2)}) async-start(), calls=%async_computation.19 | async-start | bytes 5242880 | tf_op jit(solution)/shard_map/reduce_scatter | solution.py:304
  1045.8 210.5 %reduce-scatter.21.cloned.1.call-start = ((), (), s32[]{:S(2)}) async-start(), calls=%async_computation.18 | async-start | bytes 5242880 | tf_op jit(solution)/shard_map/reduce_scatter | solution.py:304
  1074.4 252.2 %collective-permute-start.28 = (f32[2,256,2048]{2,1,0:T(8,128)}, f32[2,256,2048]{2,1,0:T(8,128)}, u32[]{:S(2)}, u32[]{:S(2)}) collective-permute-start(f32[2,256,2048]{2,1,0:T(8,128)} %bitcast.313), channel_id=1, source_target_pairs={{0,16},{1,17},{2,18},{3,19},{4,20},{5,21},{6,22},{7,23},{8,24},{9,... | collective-permute-start | bytes 12582920 | tf_op jit(solution)/shard_map/ppermute | solution.py:14
  1107.6 219.0 %collective-permute-start.27 = (f32[2,256,2048]{2,1,0:T(8,128)}, f32[2,256,2048]{2,1,0:T(8,128)}, u32[]{:S(2)}, u32[]{:S(2)}) collective-permute-start(f32[2,256,2048]{2,1,0:T(8,128)} %bitcast.68), channel_id=1, source_target_pairs={{16,0},{17,1},{18,2},{19,3},{20,4},{21,5},{22,6},{23,7},{24,8},{25... | collective-permute-start | bytes 12582920 | tf_op jit(solution)/shard_map/ppermute | solution.py:14
  1146.7 162.6 %collective-permute-start.30 = (f32[512,2,384]{2,0,1:T(8,128)}, f32[512,2,384]{2,0,1:T(8,128)}, u32[]{:S(2)}, u32[]{:S(2)}) collective-permute-start(f32[512,2,384]{2,0,1:T(8,128)} %convert_element_type.426), channel_id=1, source_target_pairs={{16,0},{17,1},{18,2},{19,3},{20,4},{21,5},{22,6},{23,7},{24,8},{25... | collective-permute-start | bytes 4718600 | tf_op jit(solution)/shard_map/ppermute | solution.py:14
  1202.7 113.0 %collective-permute-start.36 = (f32[1024,512]{1,0:T(8,128)}, f32[1024,512]{1,0:T(8,128)}, u32[]{:S(2)}, u32[]{:S(2)}) collective-permute-start(f32[1024,512]{1,0:T(8,128)} %convert_element_type.438), channel_id=1, source_target_pairs={{16,0},{17,1},{18,2},{19,3},{20,4},{21,5},{22,6},{23,7},{24,8},{25... | collective-permute-start | bytes 6291464 | tf_op jit(solution)/shard_map/ppermute | solution.py:14
  1259.0 62.1 %collective-permute-start.34 = (f32[512,1024]{1,0:T(8,128)}, f32[512,1024]{1,0:T(8,128)}, u32[]{:S(2)}, u32[]{:S(2)}) collective-permute-start(f32[512,1024]{1,0:T(8,128)} %convert_element_type.434), channel_id=1, source_target_pairs={{16,0},{17,1},{18,2},{19,3},{20,4},{21,5},{22,6},{23,7},{24,8},{25... | collective-permute-start | bytes 6291464 | tf_op jit(solution)/shard_map/ppermute | solution.py:14
  (125 other events, 3084.4 us)
Sparse Core Ops, SparseCore 0:
  9.9 72.8 all-gather.10
  84.7 90.8 all-gather.14
  177.4 87.4 all-gather.16
  266.6 35.1 all-gather.12
  380.3 93.2 all-reduce.4
  583.6 89.7 all-reduce.6
  676.9 26.6 reduce-scatter.10
  706.1 86.4 all-reduce.8
  795.6 51.8 reduce-scatter.14
  851.1 53.0 reduce-scatter.8
  907.5 70.8 reduce-scatter.12
  981.7 27.7 reduce-scatter.18
  1012.1 86.4 all-reduce.10
  1101.4 42.9 reduce-scatter.16
  1147.2 52.6 reduce-scatter.22
  1203.5 52.6 reduce-scatter.20
